TPU v7x, 32 devices: a whole 2x2x4 slice. The times are simulated.
32 devices in a mesh: vol: 8 (over z, x), rep: 4 (over y, core).
Axes of the slice: x: 2, y: 2, z: 4, core: 2. Of those that a mesh axis runs over, the one named last changes fastest.
Arguments:
- cutouts: bfloat16 [4, 256, 4096], P('rep', 'vol'), may hold values from -6 to 6
- counts: int32 [4, 8], P('rep', 'vol'), may hold values from 1 to 32, as said below
- partner: int32 [4, 128], P('rep'), may hold values from 0 to 127, as said below
- w_stem: bfloat16 [64, 128], replicated, may hold values from -0.75 to 0.75
- w_mix: bfloat16 [128, 128], replicated, may hold values from -0.5 to 0.5
- w_out: bfloat16 [128, 128], replicated, may hold values from -0.5 to 0.5
- w_proj: bfloat16 [128, 64], replicated, may hold values from -0.5 to 0.5
Outputs:
- upd_stem: float32 [64, 128], replicated
- upd_mix: float32 [128, 128], replicated
- upd_out: float32 [128, 128], replicated
- upd_proj: float32 [128, 64], replicated
- node_loss: float32 [4, 8, 16], P('rep', 'vol')
Inputs may be any that keep to these rules, and one draw needn't show every extreme that they name: `counts`: each row sums to 128, and its largest entry is exactly 32. Each row pairs the nodes of a group: partner[r, partner[r, g]] = g and partner[r, g] != g.
All inputs are finite; a program needn't handle non-finite values.
Results may differ from a plain program's by a relative error of at most 0.0035.
Values may be sent and summed in bfloat16 or wider, within the bound.
No kernel may reach another device: no remote copies, remote signals or barrier semaphores. Data moves between devices by JAX's collectives and lax.ppermute only.
A program may use at most 64 MiB of HBM per device.

v0:
```python
import jax
import jax.numpy as jnp
from jax import lax
from jax.sharding import PartitionSpec as P

logit_divisor_factor = 0.2
norm_eps = 1e-06
rms_eps = 1e-06


def prefix(part, axis, combine, identity):
    place = lax.axis_index(axis)
    gathered = lax.all_gather(part, axis)
    state = jnp.zeros_like(part) + jnp.asarray(identity, part.dtype)

    def one(lap, state):
        return combine(state, lax.dynamic_index_in_dim(gathered, lap, 0, False))

    return lax.fori_loop(0, place, one, state)


def first_dot(left, right):
    return lax.dot_general(
        left, right, (((0,), (0,)), ((), ())), preferred_element_type=jnp.float32
    )


def concluding_matrix_multiply(left, right):
    return lax.dot_general(
        left, right, (((1,), (1,)), ((), ())), preferred_element_type=jnp.float32
    )


def silu_slope(value):
    sigma = jax.nn.sigmoid(value)
    return sigma * (1.0 + value * (1.0 - sigma))


def encode(cutout_rows, w_stem, w_mix, w_out, w_proj):
    number = cutout_rows.shape[0]
    patches = cutout_rows.reshape(-1, w_stem.shape[0])
    per_cutout = patches.shape[0] // number
    pre_stem = jnp.dot(patches, w_stem, preferred_element_type=jnp.float32)
    hidden = jax.nn.silu(pre_stem).astype(jnp.bfloat16)
    pre_mix = jnp.dot(hidden, w_mix, preferred_element_type=jnp.float32)
    mixed = jax.nn.silu(pre_mix).astype(jnp.bfloat16)
    summed = hidden.astype(jnp.float32) + jnp.dot(mixed, w_out, preferred_element_type=jnp.float32)
    pooled = jnp.mean(summed.reshape(number, per_cutout, -1), axis=1).astype(jnp.bfloat16)
    raw_embed = jnp.dot(pooled, w_proj, preferred_element_type=jnp.float32)
    inv_norm = lax.rsqrt(jnp.sum(raw_embed * raw_embed, axis=1, keepdims=True) + norm_eps)
    unit_embed = raw_embed * inv_norm
    return (unit_embed, (patches, pre_stem, hidden, pre_mix, mixed, pooled, unit_embed, inv_norm))


def backward(feature_vector_derivative, saved, w_mix, w_out, w_proj):
    patches, pre_stem, hidden, pre_mix, mixed, pooled, unit_embed, inv_norm = saved
    number = pooled.shape[0]
    per_cutout = patches.shape[0] // number
    channels = hidden.shape[1]
    radial = jnp.sum(unit_embed * feature_vector_derivative, axis=1, keepdims=True)
    grad_raw = (inv_norm * (feature_vector_derivative - unit_embed * radial)).astype(jnp.bfloat16)
    grad_proj = first_dot(pooled, grad_raw)
    grad_pool = (concluding_matrix_multiply(grad_raw, w_proj) / per_cutout).astype(jnp.bfloat16)
    mixed_sum = jnp.sum(mixed.reshape(number, per_cutout, channels), axis=1, dtype=jnp.float32)
    grad_out = lax.dot_general(
        mixed_sum,
        grad_pool.astype(jnp.float32),
        (((0,), (0,)), ((), ())),
        precision=lax.Precision.HIGHEST,
        preferred_element_type=jnp.float32,
    )
    grad_mixed = concluding_matrix_multiply(grad_pool, w_out)
    mix_slope = silu_slope(pre_mix).reshape(number, per_cutout, channels)
    grad_pre_mix = (grad_mixed[:, None, :] * mix_slope).reshape(-1, channels).astype(jnp.bfloat16)
    grad_mix = first_dot(hidden, grad_pre_mix)
    spread_pool = jnp.broadcast_to(
        grad_pool.astype(jnp.float32)[:, None, :], (number, per_cutout, channels)
    ).reshape(-1, channels)
    grad_hidden = spread_pool + concluding_matrix_multiply(grad_pre_mix, w_mix)
    grad_pre_stem = (grad_hidden * silu_slope(pre_stem)).astype(jnp.bfloat16)
    grad_stem = first_dot(patches, grad_pre_stem)
    return (grad_stem, grad_mix, grad_out, grad_proj)


def contrast(anchor_feature_matrix, whole_feature_matrix, self_pos, pair_pos):
    cosine_affinity_matrix = (
        concluding_matrix_multiply(anchor_feature_matrix, whole_feature_matrix)
        / logit_divisor_factor
    )
    columns = lax.broadcasted_iota(jnp.int32, cosine_affinity_matrix.shape, 1)
    exp_scores = jnp.where(columns == self_pos[:, None], 0.0, jnp.exp(cosine_affinity_matrix))
    log_total = jnp.log(jnp.sum(exp_scores, axis=1))
    companion_feature_vector = jnp.take(whole_feature_matrix, pair_pos, axis=0).astype(jnp.float32)
    positive_couple_affinity = (
        jnp.sum(anchor_feature_matrix.astype(jnp.float32) * companion_feature_vector, axis=1)
        / logit_divisor_factor
    )
    return (exp_scores, log_total, companion_feature_vector, log_total - positive_couple_affinity)


def add_counts(earlier, later):
    return earlier + later


def locate(recv_ids, node_rank, slot_index):
    matches = recv_ids[None, :] == node_rank[:, None]
    from_slot = jnp.sum(jnp.where(matches, slot_index[None, :], 0), axis=1)
    return (matches, from_slot)


def on_device(cutouts, counts, partner, w_stem, w_mix, w_out, w_proj):
    vol_size = lax.axis_size("vol")
    vol_index = lax.axis_index("vol")
    max_nodes = cutouts.shape[1]
    node_dev = partner.shape[1] // vol_size
    capacity = (max_nodes + vol_size - 1) // vol_size
    own_cutouts = cutouts[0]
    own_count = counts[0, 0]
    offset = prefix(counts, "vol", add_counts, jnp.zeros_like(counts))[0, 0]
    slot_index = jnp.arange(vol_size * capacity, dtype=jnp.int32)
    target = slot_index // capacity
    first_rank = (offset - target + vol_size - 1) // vol_size
    slot_rank = first_rank + slot_index % capacity
    local_slot = slot_rank * vol_size + target - offset
    is_live = local_slot < own_count
    local_safe = jnp.clip(local_slot, 0, max_nodes - 1)
    send_ids = jnp.where(is_live, slot_rank, -1).astype(jnp.int32)
    node_rank = jnp.arange(node_dev, dtype=jnp.int32)
    packed = jnp.where(
        is_live[:, None], jnp.take(own_cutouts, local_safe, axis=0), jnp.zeros((), jnp.bfloat16)
    )
    arrived, recv_ids = (
        lax.all_to_all(packed, "vol", split_axis=0, concat_axis=0, tiled=True),
        lax.all_to_all(send_ids, "vol", split_axis=0, concat_axis=0, tiled=True),
    )
    matches, from_slot = locate(recv_ids, node_rank, slot_index)
    unit_embed, saved = encode(jnp.take(arrived, from_slot, axis=0), w_stem, w_mix, w_out, w_proj)
    anchor_feature_matrix = unit_embed.astype(jnp.bfloat16)
    whole_feature_matrix = lax.all_gather(anchor_feature_matrix, "vol", axis=0, tiled=True)
    self_pos = vol_index * node_dev + node_rank
    node_global = node_rank * vol_size + vol_index
    pair_global = jnp.take(partner[0], node_global)
    pair_pos = pair_global % vol_size * node_dev + pair_global // vol_size
    exp_scores, log_total, companion_feature_vector, node_loss = contrast(
        anchor_feature_matrix, whole_feature_matrix, self_pos, pair_pos
    )
    row_weight = (exp_scores * jnp.exp(-log_total)[:, None]).astype(jnp.bfloat16)
    horizontal_objective_term = jnp.dot(
        row_weight, whole_feature_matrix, preferred_element_type=jnp.float32
    )
    all_totals = lax.all_gather(log_total, "vol", axis=0, tiled=True)
    column_weight = (exp_scores * jnp.exp(-all_totals)[None, :]).astype(jnp.bfloat16)
    vertical_objective_term = jnp.dot(
        column_weight, whole_feature_matrix, preferred_element_type=jnp.float32
    )
    feature_vector_derivative = (
        horizontal_objective_term + vertical_objective_term - 2.0 * companion_feature_vector
    ) / logit_divisor_factor
    grads = backward(feature_vector_derivative, saved, w_mix, w_out, w_proj)
    grad_totals = lax.psum((grads[0], grads[1], grads[2], grads[3]), ("vol", "rep"))
    updates = [
        summed_grad * lax.rsqrt(jnp.mean(summed_grad * summed_grad) + rms_eps)
        for summed_grad in grad_totals
    ]
    return (updates[0], updates[1], updates[2], updates[3], node_loss[None, None, :])


def solution(mesh):
    in_specs = (P("rep", "vol", None), P("rep", "vol"), P("rep", None), P(), P(), P(), P())
    out_specs = (P(), P(), P(), P(), P("rep", "vol", None))
    return jax.shard_map(
        on_device, mesh=mesh, in_specs=in_specs, out_specs=out_specs, check_vma=False
    )
```

profile of v0, /device:TPU:0, one launch (start us, length us, event | category | flops | bytes accessed | tf_op | source)
XLA Modules:
  0.0 372.9 jit_solution(8634578186639433932)
XLA Ops:
  7.2 0.0 copy-start
  7.2 0.0 copy-start.10
  7.9 0.6 dynamic-slice
  8.5 0.7 bitcast_dynamic-update-slice_fusion
  9.2 13.1 %all-reduce = s32[8]{0:T(128)S(1)} all-reduce(s32[8]{0:T(128)S(1)} %bitcast_dynamic-update-slice_fusion), channel_id=2, replica_groups=mesh['vol'=8,'rep'=4] {'vol'}, use_global_device_ids=true, to_apply=%add | all-reduce | flops 8 | bytes 64
  22.3 0.6 compare_select_fusion
  22.9 11.2 %all-to-all-start = ((s32[8,4,1]{1,2,0:T(1,128)}), s32[8,4,1]{1,2,0:T(1,128)S(1)}, u32[]{:S(2)}, u32[]{:S(2)}) async-start(s32[8,4,1]{1,2,0:T(1,128)} %compare_select_fusion), calls=%async_computation | async-start | bytes 8192 | tf_op jit(solution)/shard_map/all_to_all | solution.py:134
  34.2 0.6 copy-done.1
  34.8 0.7 gather_fusion.2
  35.6 0.7 gather_fusion
  36.3 0.1 gather.23
  36.5 0.9 select_select_fusion
  38.0 2.5 all-to-all-done
  40.6 3.5 all-to-all-start.1
  44.1 0.0 all-reduce.7.cloned.1.call-start
  44.1 0.5 broadcast.952
  44.6 0.7 reduce.3
  45.3 0.1 eq.27
  45.4 0.1 select_reduce_fusion
  45.5 0.1 broadcast_in_dim.85
  45.6 0.1 broadcast_in_dim.86
  45.7 6.6 %all-to-all-done.1 = bf16[8,4,4096]{2,1,0:T(4,128)(2,1)S(1)} async-done(((bf16[8,4,4096]{2,1,0:T(4,128)(2,1)}), bf16[8,4,4096]{2,1,0:T(4,128)(2,1)S(1)}, u32[]{:S(2)}, u32[]{:S(2)}) %all-to-all-start.1) | async-done | bytes 262176 | tf_op jit(solution)/shard_map/all_to_all | solution.py:133
  52.3 0.1 all_to_all.12
  52.4 0.6 gather_fusion.1
  53.0 0.2 gather.25
  53.3 0.5 copy-done.9
  53.7 0.9 multiply_convert_fusion.1
  54.7 0.3 convert_reduce_fusion
  55.0 0.4 copy-done.7
  55.4 0.2 bitcast_reduce_fusion
  55.6 0.5 copy-done.6
  56.1 0.2 multiply_reduce_fusion.5
  56.4 0.1 multiply_convert_fusion.6
  56.4 30.6 %all_gather.14 = bf16[128,64]{1,0:T(8,128)(2,1)S(1)} all-gather(bf16[16,64]{1,0:T(8,128)(2,1)S(1)} %multiply_convert_fusion.6), channel_id=1, replica_groups=mesh['vol'=8,'rep'=4] {'vol'}, dimensions={0}, use_global_device_ids=true | all-gather | bytes 18432 | tf_op jit(solution)/shard_map/all_gather | solution.py:139
  87.1 0.6 gather_fusion.3
  87.6 0.3 fusion.49
  87.9 0.2 fusion.15
  88.1 0.5 subtract_bitcast_fusion
  88.6 18.7 %all-reduce.1 = f32[128]{0:T(128)S(1)} all-reduce(f32[128]{0:T(128)S(1)} %get-tuple-element.60), channel_id=1, replica_groups=mesh['vol'=8,'rep'=4] {'vol'}, use_global_device_ids=true, to_apply=%add.1 | all-reduce | flops 128 | bytes 1024
  107.3 0.2 fusion.22
  107.5 0.2 multiply_reduce_fusion.4
  107.8 0.1 multiply_convert_fusion.2
  107.9 0.1 fusion.7
  108.0 0.8 fusion.31
  108.8 0.1 fusion.50
  108.9 0.2 fusion.8
  109.2 0.9 fusion.51
  110.1 1.1 fusion.2
  111.2 0.0 all-reduce.7.cloned.1.call-update
  111.2 0.0 all-reduce.9.cloned.1.call-start
  111.3 0.9 fusion.52
  112.2 0.0 all-reduce.9.cloned.1.call-update
  112.2 116.4 %all-reduce.7.cloned.1.call-done = (f32[64,128]{1,0:T(8,128)}, f32[128,64]{0,1:T(8,128)}) async-done(((f32[64,128]{1,0:T(8,128)}, f32[128,64]{0,1:T(8,128)}), (f32[64,128]{1,0:T(8,128)}, f32[128,64]{0,1:T(8,128)})) %all-reduce.7.cloned.1.call-update) | async-done | bytes 65552 | tf_op jit(solution)/shard_map/psum | solution.py:160
  228.6 1.4 multiply_reduce_fusion.2
  230.7 0.6 multiply_reduce_fusion.3
  232.0 0.6 broadcast_multiply_fusion.3
  232.6 0.1 copy-done.4
  232.8 0.6 broadcast_multiply_fusion.2
  233.4 127.7 %all-reduce.9.cloned.1.call-done = (f32[128,128]{1,0:T(8,128)}, f32[128,128]{1,0:T(8,128)}) async-done(((f32[128,128]{1,0:T(8,128)}, f32[128,128]{1,0:T(8,128)}), (f32[128,128]{1,0:T(8,128)}, f32[128,128]{1,0:T(8,128)})) %all-reduce.9.cloned.1.call-update) | async-done | bytes 131088 | tf_op jit(solution)/shard_map/psum | solution.py:160
  361.1 1.5 multiply_reduce_fusion
  363.3 0.6 multiply_reduce_fusion.1
  364.6 0.6 broadcast_multiply_fusion.1
  365.2 0.2 copy-done.2
  365.4 0.6 broadcast_multiply_fusion
  (32 shorter events, 0.2 us)
Async XLA Ops:
  7.2 28.5 %copy-start = (bf16[1,32,4096]{2,1,0:T(8,128)(2,1)S(1)}, bf16[1,32,4096]{2,1,0:T(8,128)(2,1)}, u32[]{:S(2)}) copy-start(bf16[1,32,4096]{2,1,0:T(8,128)(2,1)} %param.9) | copy-start | bytes 786436
  7.2 0.7 copy-start.10
  22.9 17.6 %all-to-all-start = ((s32[8,4,1]{1,2,0:T(1,128)}), s32[8,4,1]{1,2,0:T(1,128)S(1)}, u32[]{:S(2)}, u32[]{:S(2)}) async-start(s32[8,4,1]{1,2,0:T(1,128)} %compare_select_fusion), calls=%async_computation | async-start | bytes 8192 | tf_op jit(solution)/shard_map/all_to_all | solution.py:134
  34.2 0.7 copy-start.1
  40.6 11.7 %all-to-all-start.1 = ((bf16[8,4,4096]{2,1,0:T(4,128)(2,1)}), bf16[8,4,4096]{2,1,0:T(4,128)(2,1)S(1)}, u32[]{:S(2)}, u32[]{:S(2)}) async-start(bf16[8,4,4096]{2,1,0:T(4,128)(2,1)} %select_select_fusion), calls=%async_computation.1 | async-start | bytes 524288 | tf_op jit(solution)/shard_map/all_to_all | solution.py:133
  44.1 184.6 %all-reduce.7.cloned.1.call-start = ((), (), s32[]{:S(2)}) async-start(), calls=%async_computation.2 | async-start | bytes 131072 | tf_op jit(solution)/shard_map/psum | solution.py:160
  53.0 0.7 copy-start.9
  53.7 0.9 copy-start.8
  54.6 0.8 copy-start.7
  55.4 0.7 copy-start.6
  111.2 249.8 %all-reduce.9.cloned.1.call-start = ((), (), s32[]{:S(2)}) async-start(), calls=%async_computation.3 | async-start | bytes 262144 | tf_op jit(solution)/shard_map/psum | solution.py:160
  228.6 2.1 copy-start.5
  232.0 0.8 copy-start.4
  361.1 2.2 copy-start.3
  364.6 0.8 copy-start.2
Sparse Core Ops, SparseCore 0:
  111.4 117.2 all-reduce.6
  234.9 126.0 all-reduce.8
where the time goes:
time: 374 us; the launch traced here: 373 us
  waiting for transfers between devices  253 us (68%)
  blocking collectives  62.4 us (17%)
  between operations  18.4 us (5%)
  starting transfers between devices  14.8 us (4%)
  other arithmetic  10.2 us (3%)
  local copies, waits for them, and re-layouts  7.41 us (2%)
  matrix products  6.33 us (2%)
    psum x2, waiting for transfers between devices, on_device(): lax.psum((grads[0], grads[1], grads[2], grads[3]), ('vol', 'rep'))  244 us
    unnamed x2, blocking collectives  31.8 us
    all_gather x1, blocking collectives, on_device(): lax.all_gather(anchor_feature_matrix, 'vol', axis=0, tiled=True)  30.6 us
    all_to_all x1, starting transfers between devices, on_device(): lax.all_to_all(send_ids, 'vol', split_axis=0, concat_axis=0, tiled=True)  11.2 us
  transfers between devices with their start and end apart: 4, of which 4 were waited for; matrix products, arithmetic and copies ran while one was open for 2% of the time, Pallas kernels for 0%

commit v1 on v0

v1 whole, which is shorter than its diff:
```python
import jax
import jax.numpy as jnp
from jax import lax
from jax.experimental import pallas as pl
from jax.experimental.pallas import tpu as pltpu
from jax.sharding import PartitionSpec as P

TEMPERATURE = 0.2
NORM_EPS = 1e-06
RMS_EPS = 1e-06
BF16 = jnp.bfloat16
F32 = jnp.float32
GROUP = 4


def nn(left, right):
    return lax.dot_general(left, right, (((1,), (0,)), ((), ())), preferred_element_type=F32)


def nt(left, right):
    return lax.dot_general(left, right, (((1,), (1,)), ((), ())), preferred_element_type=F32)


def tn(left, right):
    return lax.dot_general(left, right, (((0,), (0,)), ((), ())), preferred_element_type=F32)


def sigmoid(value):
    return 0.5 + 0.5 * jnp.tanh(0.5 * value)


def split(value):
    high = value.astype(BF16)
    low = (value - high.astype(F32)).astype(BF16)
    return high, low


def paired(weight):
    zero = jnp.zeros_like(weight)
    return jnp.concatenate(
        [
            jnp.concatenate([weight, zero], axis=1),
            jnp.concatenate([zero, weight], axis=1),
        ],
        axis=0,
    )


def pair_rows(cut_ref, width, first, number):
    return jnp.concatenate(
        [cut_ref[:, (first + i) * width : (first + i + 1) * width] for i in range(number)], axis=0
    )


def forward_kernel(
    count_ref, cut_ref, stem_ref, mix_ref, out_ref, proj_ref,
    send_ref, pooled_ref, mixed_ref, unit_ref, inv_ref,
):
    nodes = cut_ref.shape[0]
    voxels, channels = stem_ref.shape
    width = 2 * voxels
    blocks = cut_ref.shape[1] // width
    stem2 = paired(stem_ref[...])
    mix2 = paired(mix_ref[...])
    hidden_sum = jnp.zeros((nodes, 2 * channels), F32)
    mixed_sum = jnp.zeros((nodes, 2 * channels), F32)
    for first in range(0, blocks, GROUP):
        number = min(GROUP, blocks - first)
        pre_stem = nn(pair_rows(cut_ref, width, first, number), stem2)
        hidden = (pre_stem * sigmoid(pre_stem)).astype(BF16)
        pre_mix = nn(hidden, mix2)
        mixed = (pre_mix * sigmoid(pre_mix)).astype(BF16)
        for i in range(number):
            rows = slice(i * nodes, (i + 1) * nodes)
            hidden_sum = hidden_sum + hidden[rows].astype(F32)
            mixed_sum = mixed_sum + mixed[rows].astype(F32)
    hidden_sum = hidden_sum[:, :channels] + hidden_sum[:, channels:]
    mixed_sum = mixed_sum[:, :channels] + mixed_sum[:, channels:]
    high, low = split(mixed_sum)
    weight = out_ref[...]
    summed = hidden_sum + (nn(high, weight) + nn(low, weight))
    pooled = (summed / (2 * blocks)).astype(BF16)
    raw = nn(pooled, proj_ref[...])
    inv = lax.rsqrt(jnp.sum(raw * raw, axis=1, keepdims=True) + NORM_EPS)
    unit = raw * inv
    count = count_ref[0]
    live = lax.broadcasted_iota(jnp.int32, unit.shape, 0) < count
    embed = jnp.where(live, unit, 0.0)
    counts = jnp.zeros(unit.shape, F32) + count.astype(F32)
    send_ref[...] = jnp.concatenate([embed, counts], axis=1).astype(BF16)
    pooled_ref[...] = pooled
    mixed_ref[...] = mixed_sum
    unit_ref[...] = unit
    inv_ref[...] = inv


def slope_kernel(
    send_ref, cut_ref, stem_ref, mix_ref, hidden_t_ref, patch_t_ref, stem_slope_ref, mix_slope_ref
):
    nodes = cut_ref.shape[0]
    voxels = stem_ref.shape[0]
    width = 2 * voxels
    blocks = cut_ref.shape[1] // width
    stem2 = paired(stem_ref[...])
    mix2 = paired(mix_ref[...])
    for first in range(0, blocks, GROUP):
        number = min(GROUP, blocks - first)
        rows = slice(first * nodes, (first + number) * nodes)
        patches = pair_rows(cut_ref, width, first, number)
        pre_stem = nn(patches, stem2)
        sigma = sigmoid(pre_stem)
        scaled = pre_stem * sigma
        hidden = scaled.astype(BF16)
        stem_slope_ref[rows, :] = sigma + scaled * (1.0 - sigma)
        pre_mix = nn(hidden, mix2)
        sigma = sigmoid(pre_mix)
        mix_slope_ref[rows, :] = sigma + pre_mix * sigma * (1.0 - sigma)
        hidden_t_ref[:, rows] = hidden.T
        patch_t_ref[:, rows] = patches.T


def slot_tables(gathered_ref, embed_dim, max_nodes):
    slots = gathered_ref.shape[0]
    owners = slots // max_nodes
    lane = lax.broadcasted_iota(jnp.int32, (8, gathered_ref.shape[1]), 1)
    pick = jnp.where(lane == embed_dim, 1.0, 0.0).astype(BF16)
    count = nt(pick, gathered_ref[...])
    slot = lax.broadcasted_iota(jnp.int32, (8, slots), 1)
    heads = jnp.where(slot % max_nodes == 0, count, 0.0)
    step = min(slots, 512)
    row = lax.broadcasted_iota(jnp.int32, (step, slots), 0)
    column_owner = lax.broadcasted_iota(jnp.int32, (step, slots), 1) // max_nodes
    offset = jnp.zeros((8, slots), F32)
    for first in range(0, slots, step):
        earlier = jnp.where((row + first) // max_nodes < column_owner, 1.0, 0.0).astype(BF16)
        offset = offset + nn(heads[:, first : first + step].astype(BF16), earlier)
    del owners
    return count[0:1], offset[0:1], heads[0:1]


def score_sums(gathered_ref, embed_dim, max_nodes, live_row):
    slots = gathered_ref.shape[0]
    step = min(slots, 256)
    whole = gathered_ref[:, :embed_dim]

    def block(first, total):
        part = gathered_ref[pl.ds(first, step), :]
        scores = nt(part[:, :embed_dim], whole) / TEMPERATURE
        count = part[:, embed_dim : embed_dim + 1].astype(F32)
        row = lax.broadcasted_iota(jnp.int32, (step, 1), 0) + first
        live = (row % max_nodes).astype(F32) < count
        column = lax.broadcasted_iota(jnp.int32, scores.shape, 1)
        keep = jnp.logical_and(live, column != row)
        return total + jnp.sum(jnp.where(keep, jnp.exp(scores), 0.0), axis=0, keepdims=True)

    total = jnp.zeros((1, slots), F32)
    if slots == step:
        total = block(0, total)
    else:
        total = lax.fori_loop(
            0, slots // step, lambda i, t: block(pl.multiple_of(i * step, step), t), total
        )
    return jnp.where(live_row, total, 1.0)


def backward_kernel(
    place_ref, gathered_ref, partner_ref, send_ref, pooled_ref, mixed_ref, unit_ref, inv_ref,
    hidden_t_ref, patch_t_ref, stem_slope_ref, mix_slope_ref, mix_ref, out_ref, proj_ref, grad_ref,
):
    nodes, embed_dim = unit_ref.shape
    slots = gathered_ref.shape[0]
    place = place_ref[0]
    own_count = place_ref[1]
    channels = mix_ref.shape[0]
    voxels = patch_t_ref.shape[0] // 2
    blocks = stem_slope_ref.shape[0] // nodes

    count_row, offset_row, heads = slot_tables(gathered_ref, embed_dim, nodes)
    slot_row = lax.broadcasted_iota(jnp.int32, (1, slots), 1)
    within = (slot_row % nodes).astype(F32)
    live_row = within < count_row
    number_row = jnp.where(live_row, offset_row + within, -1.0)
    totals = score_sums(gathered_ref, embed_dim, nodes, live_row)

    own_offset = jnp.sum(
        jnp.where(slot_row // nodes < place, heads, 0.0), axis=1, keepdims=True
    )
    rank = lax.broadcasted_iota(jnp.int32, (nodes, 1), 0)
    own_live = rank < own_count
    own_number = own_offset + rank.astype(F32)
    partner = partner_ref[...].astype(F32)
    listed = lax.broadcasted_iota(jnp.int32, (nodes, partner.shape[1]), 1).astype(F32)
    mate = jnp.sum(jnp.where(listed == own_number, partner, 0.0), axis=1, keepdims=True)
    companion = jnp.where(number_row == mate, 1.0, 0.0).astype(BF16)

    whole = gathered_ref[:, :embed_dim]
    scores = nt(send_ref[:, :embed_dim], whole) / TEMPERATURE
    other = jnp.logical_and(live_row, slot_row != rank + place * nodes)
    weight = jnp.where(other, jnp.exp(scores), 0.0)
    own_total = jnp.sum(weight, axis=1, keepdims=True)
    row_weight = (weight * (1.0 / own_total)).astype(BF16)
    column_weight = (weight * (1.0 / totals)).astype(BF16)
    mixed_rows = nn(jnp.concatenate([row_weight, column_weight, companion], axis=0), whole)
    d_embed = (
        mixed_rows[:nodes] + mixed_rows[nodes : 2 * nodes] - 2.0 * mixed_rows[2 * nodes :]
    ) / TEMPERATURE

    unit = unit_ref[...]
    radial = jnp.sum(unit * d_embed, axis=1, keepdims=True)
    d_raw = jnp.where(own_live, inv_ref[...] * (d_embed - unit * radial), 0.0).astype(BF16)
    g_proj = tn(pooled_ref[...], d_raw)
    d_sum = (nt(d_raw, proj_ref[...]) / (2 * blocks)).astype(BF16)
    high, low = split(mixed_ref[...])
    g_out = tn(high, d_sum) + tn(low, d_sum)
    d_mixed = nt(d_sum, out_ref[...])
    d_mixed = jnp.concatenate([d_mixed, d_mixed], axis=1)
    d_pool = d_sum.astype(F32)
    d_pool = jnp.concatenate([d_pool, d_pool], axis=1)
    mix2 = paired(mix_ref[...])

    g_mix = jnp.zeros((2 * channels, 2 * channels), F32)
    g_stem = jnp.zeros((2 * voxels, 2 * channels), F32)
    chunk = 2 * GROUP
    for first in range(0, blocks, chunk):
        number = min(chunk, blocks - first)
        rows = slice(first * nodes, (first + number) * nodes)
        d_pre_mix = jnp.concatenate(
            [
                (d_mixed * mix_slope_ref[(first + i) * nodes : (first + i + 1) * nodes, :]).astype(BF16)
                for i in range(number)
            ],
            axis=0,
        )
        g_mix = g_mix + nn(hidden_t_ref[:, rows], d_pre_mix)
        back = nt(d_pre_mix, mix2)
        d_pre_stem = jnp.concatenate(
            [
                (
                    (d_pool + back[i * nodes : (i + 1) * nodes])
                    * stem_slope_ref[(first + i) * nodes : (first + i + 1) * nodes, :]
                ).astype(BF16)
                for i in range(number)
            ],
            axis=0,
        )
        g_stem = g_stem + nn(patch_t_ref[:, rows], d_pre_stem)
    g_mix = g_mix[:channels, :channels] + g_mix[channels:, channels:]
    g_stem = g_stem[:voxels, :channels] + g_stem[voxels:, channels:]
    half = channels // 2
    g_proj = jnp.concatenate([g_proj[:half], g_proj[half:]], axis=1)
    grad_ref[...] = jnp.concatenate([g_stem, g_mix, g_out, g_proj], axis=0).astype(grad_ref.dtype)


def loss_kernel(place_ref, gathered_ref, partner_ref, anchor_ref, loss_ref, *, embed_dim, max_nodes):
    slots = gathered_ref.shape[0]
    owners = slots // max_nodes
    place = place_ref[0]
    node_dev = loss_ref.shape[0]
    del anchor_ref
    count_row, offset_row, _ = slot_tables(gathered_ref, embed_dim, max_nodes)
    slot_row = lax.broadcasted_iota(jnp.int32, (1, slots), 1)
    within = (slot_row % max_nodes).astype(F32)
    live_row = within < count_row
    number_row = jnp.where(live_row, offset_row + within, -1.0)
    totals = score_sums(gathered_ref, embed_dim, max_nodes, live_row)
    number = (lax.broadcasted_iota(jnp.int32, (node_dev, 1), 0) * owners + place).astype(F32)
    partner = partner_ref[...].astype(F32)
    listed = lax.broadcasted_iota(jnp.int32, (node_dev, partner.shape[1]), 1).astype(F32)
    mate = jnp.sum(jnp.where(listed == number, partner, 0.0), axis=1, keepdims=True)
    mine = number_row == number
    total = jnp.sum(jnp.where(mine, totals, 0.0), axis=1, keepdims=True)
    whole = gathered_ref[:, :embed_dim]
    anchor = nn(jnp.where(mine, 1.0, 0.0).astype(BF16), whole)
    companion = nn(jnp.where(number_row == mate, 1.0, 0.0).astype(BF16), whole)
    positive = jnp.sum(anchor * companion, axis=1, keepdims=True) / TEMPERATURE
    loss_ref[...] = jnp.broadcast_to(jnp.log(total) - positive, loss_ref.shape)


def update_kernel(grad_ref, stem_ref, mix_ref, out_ref, proj_ref):
    start = 0
    for ref in (stem_ref, mix_ref, out_ref, proj_ref):
        size = ref.shape[0] * ref.shape[1]
        rows = size // grad_ref.shape[1]
        grad = grad_ref[start : start + rows, :].astype(F32)
        start += rows
        squares = jnp.sum(jnp.sum(grad * grad, axis=0, keepdims=True), axis=1, keepdims=True)
        update = grad * lax.rsqrt(squares / size + RMS_EPS)
        if ref.shape[1] == grad_ref.shape[1]:
            ref[...] = update
        else:
            half = ref.shape[1]
            ref[:rows, :] = update[:, :half]
            ref[rows:, :] = update[:, half:]


def vmem(number):
    return [pl.BlockSpec(memory_space=pltpu.VMEM)] * number


def smem():
    return pl.BlockSpec(memory_space=pltpu.SMEM)


def on_device(cutouts, counts, partner, w_stem, w_mix, w_out, w_proj):
    axes = ("vol", "rep")
    owners = lax.axis_size("vol")
    devices = owners * lax.axis_size("rep")
    place = lax.axis_index("vol").astype(jnp.int32)
    cut = cutouts[0]
    nodes = cut.shape[0]
    voxels, channels = w_stem.shape
    embed_dim = w_proj.shape[1]
    rows = cut.shape[1] // (2 * voxels) * nodes
    own_count = counts[0]
    shape = jax.ShapeDtypeStruct

    send, pooled, mixed_sum, unit, inv = pl.pallas_call(
        forward_kernel,
        out_shape=(
            shape((nodes, 2 * embed_dim), BF16),
            shape((nodes, channels), BF16),
            shape((nodes, channels), F32),
            shape((nodes, embed_dim), F32),
            shape((nodes, 1), F32),
        ),
        in_specs=[smem()] + vmem(5),
        out_specs=tuple(vmem(5)),
    )(own_count, cut, w_stem, w_mix, w_out, w_proj)

    gathered = lax.all_to_all(
        jnp.broadcast_to(send[None], (owners,) + send.shape), "vol", 0, 0
    ).reshape(owners * nodes, 2 * embed_dim)

    hidden_t, patch_t, stem_slope, mix_slope = pl.pallas_call(
        slope_kernel,
        out_shape=(
            shape((2 * channels, rows), BF16),
            shape((2 * voxels, rows), BF16),
            shape((rows, 2 * channels), F32),
            shape((rows, 2 * channels), F32),
        ),
        in_specs=vmem(4),
        out_specs=tuple(vmem(4)),
    )(send, cut, w_stem, w_mix)

    where = jnp.stack([place, own_count[0]])
    total_rows = (w_stem.size + w_mix.size + w_out.size + w_proj.size) // channels
    grad = pl.pallas_call(
        backward_kernel,
        out_shape=shape((total_rows, channels), BF16),
        in_specs=[smem()] + vmem(14),
        out_specs=vmem(1)[0],
    )(
        where, gathered, partner, send, pooled, mixed_sum, unit, inv,
        hidden_t, patch_t, stem_slope, mix_slope, w_mix, w_out, w_proj,
    )

    share = (total_rows + devices - 1) // devices
    if share * devices != total_rows:
        grad = jnp.pad(grad, ((0, share * devices - total_rows), (0, 0)))
    parts = lax.all_to_all(grad.reshape(devices, share, channels), axes, 0, 0)
    mine = jnp.sum(parts.astype(F32), axis=0).astype(BF16)
    whole = lax.all_to_all(jnp.broadcast_to(mine[None], (devices,) + mine.shape), axes, 0, 0)
    whole = whole.reshape(devices * share, channels)[:total_rows]

    node_dev = partner.shape[1] // owners
    loss = pl.pallas_call(
        lambda *refs: loss_kernel(*refs, embed_dim=embed_dim, max_nodes=nodes),
        out_shape=shape((node_dev, 128), F32),
        in_specs=[smem()] + vmem(2) + [pl.BlockSpec(memory_space=pl.ANY)],
        out_specs=vmem(1)[0],
    )(where, gathered, partner, grad)

    updates = pl.pallas_call(
        update_kernel,
        out_shape=tuple(shape(w.shape, F32) for w in (w_stem, w_mix, w_out, w_proj)),
        in_specs=vmem(1),
        out_specs=tuple(vmem(4)),
    )(whole)
    return (*updates, loss[:, 0][None, None, :])


def solution(mesh):
    in_specs = (P("rep", "vol", None), P("rep", "vol"), P("rep", None), P(), P(), P(), P())
    out_specs = (P(), P(), P(), P(), P("rep", "vol", None))
    return jax.shard_map(
        on_device, mesh=mesh, in_specs=in_specs, out_specs=out_specs, check_vma=False
    )
```

time: 374 us -> 53.5 us (0.14)
  waiting for transfers between devices: 253 us -> 8.14 us
  blocking collectives: 62.4 us -> 10.9 us
  between operations: 18.4 us -> 1.3 us
  Pallas kernels: 0 us -> 13.6 us
  other arithmetic: 10.2 us -> 0.63 us
  matrix products: 6.33 us -> 0 us
  starting transfers between devices: 14.8 us -> 9.85 us
    psum x2 -> x0, waiting for transfers between devices: 244 us -> none  [on_device(): lax.psum((grads[0], grads[1], grads[2], grads[3]), ('vol', 'rep'))]
    unnamed x2 -> x0, blocking collectives: 31.8 us -> none
    all_gather x1 -> x0, blocking collectives: 30.6 us -> none  [on_device(): lax.all_gather(anchor_feature_matrix, 'vol', axis=0, tiled=True)]
    pallas_call x0 -> x5, Pallas kernels: none -> 13.6 us  [the longest x1 4.17 us: on_device(): pl.pallas_call(backward_kernel, out_shape=shape((total_rows, channels), B...]
    all_to_all x0 -> x1, blocking collectives: none -> 10.9 us  [on_device(): parts = lax.all_to_all(grad.reshape(devices, share, channels), axes, 0, 0)]
    dot_general x13 -> x0, matrix products: 6.33 us -> none  [the longest x3 2.83 us: first_dot(): lax.dot_general(left, right, (((0,), (0,)), ((), ())), preferred_element_...]
    all_to_all x2, starting transfers between devices: 14.7 us -> 9.85 us  [the longest x1 7.28 us: on_device(): lax.all_to_all(jnp.broadcast_to(send[None], (owners,) + send.shape), 'vol...]
    reduce_sum x6 -> x1, other arithmetic: 4.39 us -> 0.04 us  [on_device(): mine = jnp.sum(parts.astype(F32), axis=0).astype(BF16)]
  transfers between devices with their start and end apart: 4 -> 2, of which waited for: 4 -> 2; matrix products, arithmetic and copies ran while one was open for 2% -> 4% of each run, Pallas kernels for 0% -> 10%
where the time goes in v1:
time: 53.5 us; the launch traced here: 52.8 us
  Pallas kernels  13.6 us (25%)
  blocking collectives  10.9 us (20%)
  starting transfers between devices  9.85 us (18%)
  local copies, waits for them, and re-layouts  8.49 us (16%)
  waiting for transfers between devices  8.14 us (15%)
  between operations  1.3 us (2%)
  other arithmetic  0.63 us (1%)
    all_to_all x1, blocking collectives, on_device(): parts = lax.all_to_all(grad.reshape(devices, share, channels), axes, 0, 0)  10.9 us
    all_to_all x1, starting transfers between devices, on_device(): lax.all_to_all(jnp.broadcast_to(send[None], (owners,) + send.shape), 'vol...  7.28 us
    all_to_all x1, waiting for transfers between devices, on_device(): lax.all_to_all(jnp.broadcast_to(mine[None], (devices,) + mine.shape), axe...  4.95 us
    pallas_call x1, Pallas kernels, on_device(): pl.pallas_call(backward_kernel, out_shape=shape((total_rows, channels), B...  4.17 us
    unnamed x4, local copies, waits for them, and re-layouts  3.6 us
    all_to_all x1, waiting for transfers between devices, on_device(): lax.all_to_all(jnp.broadcast_to(send[None], (owners,) + send.shape), 'vol...  3.19 us
    pallas_call x1, Pallas kernels, on_device(): pl.pallas_call(slope_kernel, out_shape=(shape((2 * channels, rows), BF16)...  3.12 us
    pallas_call x1, Pallas kernels, on_device(): pl.pallas_call(forward_kernel, out_shape=(shape((nodes, 2 * embed_dim), B...  2.64 us
  transfers between devices with their start and end apart: 2, of which 2 were waited for; matrix products, arithmetic and copies ran while one was open for 4% of the time, Pallas kernels for 10%

profile of v1, /device:TPU:0, one launch (start us, length us, event | category | flops | bytes accessed | tf_op | source)
XLA Modules:
  0.0 52.8 jit_solution(6736635077192943032)
XLA Ops:
  1.3 1.4 %copy.15.proj_ref = bf16[128,64]{1,0:T(8,128)(2,1)} copy(bf16[128,64]{0,1:T(8,128)(2,1)} %param.13) | data formatting | bytes 32768 | tf_op args[6]
  2.7 2.6 %shard_map.110 = (bf16[32,128]{1,0:T(8,128)(2,1)}, bf16[32,128]{1,0:T(8,128)(2,1)}, f32[32,128]{1,0:T(8,128)}, f32[32,64]{1,0:T(8,128)}, f32[32,1]{1,0:T(8,128)}) custom-call(s32[1]{0:T(128)} %bitcast.6.count_ref, bf16[32,4096]{1,0:T(8,128)(2,1)} %bitcast.7, bf16[64,128]{1,0:T(8,128)(2,1)} %stem_ref.3, bf16[128,128]{1,0:T(8,128)(2,1)} %mix_ref.5, ...), custom_call_target="tpu_custom_call" | custom-call | tf_op jit(solution)/shard_map/pallas_call | solution.py:317
  5.3 1.3 %broadcast_in_dim.4 = bf16[8,32,128]{2,1,0:T(8,128)(2,1)} broadcast(bf16[32,128]{1,0:T(8,128)(2,1)} %get-tuple-element.18.send_ref), dimensions={1,2} | broadcast | bytes 73728 | tf_op jit(solution)/shard_map/broadcast_in_dim | solution.py:331
  6.7 7.3 %all-to-all-start = ((bf16[8,32,128]{2,1,0:T(8,128)(2,1)}), bf16[8,32,128]{2,1,0:T(8,128)(2,1)S(1)}, u32[]{:S(2)}, u32[]{:S(2)}) async-start(bf16[8,32,128]{2,1,0:T(8,128)(2,1)} %broadcast_in_dim.4), calls=%async_computation | async-start | bytes 131072 | tf_op jit(solution)/shard_map/all_to_all | solution.py:330
  14.0 3.1 %shard_map.111 = (bf16[256,1024]{1,0:T(8,128)(2,1)}, bf16[128,1024]{1,0:T(8,128)(2,1)}, f32[1024,256]{1,0:T(8,128)}, f32[1024,256]{1,0:T(8,128)}) custom-call(bf16[32,128]{1,0:T(8,128)(2,1)} %get-tuple-element.18.send_ref, bf16[32,4096]{1,0:T(8,128)(2,1)} %bitcast.8, bf16[64,128]{1,0:T(8,128)(2,1)} %stem_ref.3, bf16[128,128]{1,0:T(8,128)(2,1)} %mix_ref.5), custom_call_target="tpu_custom_call" | custom-call | tf_op jit(solution)/shard_map/pallas_call | solution.py:334
  17.1 0.6 %pad_add_fusion.place_ref.refs_0_ = s32[2]{0:T(128)} fusion(s32[1]{0:T(128)} %bitcast.5, s32[1]{0:T(128)} %bitcast), kind=kLoop, calls=%fused_computation.1 | loop fusion | flops 2 | bytes 16 | tf_op jit(solution)/shard_map/stack | solution.py:346
  17.7 3.2 %all-to-all-done = bf16[8,32,128]{2,1,0:T(8,128)(2,1)S(1)} async-done(((bf16[8,32,128]{2,1,0:T(8,128)(2,1)}), bf16[8,32,128]{2,1,0:T(8,128)(2,1)S(1)}, u32[]{:S(2)}, u32[]{:S(2)}) %all-to-all-start) | async-done | bytes 65568 | tf_op jit(solution)/shard_map/all_to_all | solution.py:330
  20.9 0.0 copy-start
  20.9 0.6 %copy-done = bf16[8,32,128]{2,1,0:T(8,128)(2,1)} copy-done((bf16[8,32,128]{2,1,0:T(8,128)(2,1)}, bf16[8,32,128]{2,1,0:T(8,128)(2,1)S(1)}, u32[]{:S(2)}) %copy-start) | copy-done | bytes 65560
  21.5 4.2 %shard_map.112.refs_3_ = bf16[384,128]{1,0:T(8,128)(2,1)} custom-call(s32[2]{0:T(128)} %pad_add_fusion.place_ref.refs_0_, bf16[256,128]{1,0:T(8,128)(2,1)} %bitcast.9, s32[1,128]{1,0:T(1,128)} %refs_2_.1, bf16[32,128]{1,0:T(8,128)(2,1)} %get-tuple-element.18.send_ref, bf16[32,128]{1,0:T(8,128)(2,1)} %get-tuple-element.19.pooled_ref, ...), custom_call_target="tpu_custom_call" | custom-call | tf_op jit(solution)/shard_map/pallas_call | solution.py:348
  25.7 0.9 %reshape.22 = bf16[32,12,128]{2,1,0:T(8,128)(2,1)S(1)} reshape(bf16[384,128]{1,0:T(8,128)(2,1)} %shard_map.112.refs_3_) | data formatting | bytes 196608 | tf_op jit(solution)/shard_map/reshape | solution.py:361
  26.6 10.9 %all_to_all.15 = bf16[32,12,128]{2,1,0:T(8,128)(2,1)S(1)} all-to-all(bf16[32,12,128]{2,1,0:T(8,128)(2,1)S(1)} %reshape.22), channel_id=1, replica_groups=mesh['vol'=8,'rep'=4] {'vol','rep'}, dimensions={0} | all-to-all | bytes 196608 | tf_op jit(solution)/shard_map/all_to_all | solution.py:361
  37.5 0.7 %broadcast_in_dim.5 = bf16[32,12,128]{2,1,0:T(8,128)(2,1)} broadcast(bf16[12,128]{1,0:T(8,128)(2,1)S(1)} %reduce_sum.12), dimensions={1,2} | broadcast | bytes 101376 | tf_op jit(solution)/shard_map/broadcast_in_dim | solution.py:363
  38.2 2.6 %all-to-all-start.2 = ((bf16[32,12,128]{2,1,0:T(8,128)(2,1)}), bf16[32,12,128]{2,1,0:T(8,128)(2,1)S(1)}, u32[]{:S(2)}, u32[]{:S(2)}) async-start(bf16[32,12,128]{2,1,0:T(8,128)(2,1)} %broadcast_in_dim.5), calls=%async_computation.2 | async-start | bytes 262144 | tf_op jit(solution)/shard_map/all_to_all | solution.py:363
  40.7 1.9 %shard_map.114 = f32[16,128]{1,0:T(8,128)} custom-call(s32[2]{0:T(128)} %pad_add_fusion.place_ref.refs_0_, bf16[256,128]{1,0:T(8,128)(2,1)} %bitcast.10, s32[1,128]{1,0:T(1,128)} %refs_2_.1, bf16[384,128]{1,0:T(8,128)(2,1)} %shard_map.112.refs_3_), custom_call_target="tpu_custom_call" | custom-call | tf_op jit(solution)/shard_map/pallas_call | solution.py:367
  42.7 1.3 %slice_reduce_fusion = f32[16]{0:T(128)} fusion(f32[16,128]{1,0:T(8,128)} %shard_map.114), kind=kLoop, calls=%fused_computation | loop fusion | bytes 128 | tf_op jit(solution)/shard_map/slice | solution.py:380
  44.0 4.9 %all-to-all-done.2 = bf16[32,12,128]{2,1,0:T(8,128)(2,1)S(1)} async-done(((bf16[32,12,128]{2,1,0:T(8,128)(2,1)}), bf16[32,12,128]{2,1,0:T(8,128)(2,1)S(1)}, u32[]{:S(2)}, u32[]{:S(2)}) %all-to-all-start.2) | async-done | bytes 98336 | tf_op jit(solution)/shard_map/all_to_all | solution.py:363
  48.9 0.7 %reshape.23.grad_ref = bf16[384,128]{1,0:T(8,128)(2,1)} reshape(bf16[32,12,128]{2,1,0:T(8,128)(2,1)S(1)} %all-to-all-done.2) | data formatting | bytes 196608 | tf_op jit(solution)/shard_map/reshape | solution.py:364
  49.6 1.7 %shard_map.113 = (f32[64,128]{1,0:T(8,128)}, f32[128,128]{1,0:T(8,128)}, f32[128,128]{1,0:T(8,128)}, f32[128,64]{1,0:T(8,128)}) custom-call(bf16[384,128]{1,0:T(8,128)(2,1)} %reshape.23.grad_ref), custom_call_target="tpu_custom_call" | custom-call | tf_op jit(solution)/shard_map/pallas_call | solution.py:374
  51.3 1.5 %copy.17 = f32[128,64]{0,1:T(8,128)} copy(f32[128,64]{1,0:T(8,128)} %get-tuple-element.39) | data formatting | bytes 65536
  (1 shorter events, 0.0 us)
Async XLA Ops:
  6.7 14.2 %all-to-all-start = ((bf16[8,32,128]{2,1,0:T(8,128)(2,1)}), bf16[8,32,128]{2,1,0:T(8,128)(2,1)S(1)}, u32[]{:S(2)}, u32[]{:S(2)}) async-start(bf16[8,32,128]{2,1,0:T(8,128)(2,1)} %broadcast_in_dim.4), calls=%async_computation | async-start | bytes 131072 | tf_op jit(solution)/shard_map/all_to_all | solution.py:330
  20.9 0.6 %copy-start = (bf16[8,32,128]{2,1,0:T(8,128)(2,1)}, bf16[8,32,128]{2,1,0:T(8,128)(2,1)S(1)}, u32[]{:S(2)}) copy-start(bf16[8,32,128]{2,1,0:T(8,128)(2,1)S(1)} %all-to-all-done) | copy-start | bytes 196612
  38.2 10.8 %all-to-all-start.2 = ((bf16[32,12,128]{2,1,0:T(8,128)(2,1)}), bf16[32,12,128]{2,1,0:T(8,128)(2,1)S(1)}, u32[]{:S(2)}, u32[]{:S(2)}) async-start(bf16[32,12,128]{2,1,0:T(8,128)(2,1)} %broadcast_in_dim.5), calls=%async_computation.2 | async-start | bytes 262144 | tf_op jit(solution)/shard_map/all_to_all | solution.py:363

commit v2 on v1

--- a/solution.py
+++ b/solution.py
@@ -80,14 +80,15 @@
     weight = out_ref[...]
     summed = hidden_sum + (nn(high, weight) + nn(low, weight))
     pooled = (summed / (2 * blocks)).astype(BF16)
-    raw = nn(pooled, proj_ref[...])
+    raw = nt(pooled, proj_ref[...])
     inv = lax.rsqrt(jnp.sum(raw * raw, axis=1, keepdims=True) + NORM_EPS)
     unit = raw * inv
-    count = count_ref[0]
+    count = count_ref[...]
     live = lax.broadcasted_iota(jnp.int32, unit.shape, 0) < count
     embed = jnp.where(live, unit, 0.0)
     counts = jnp.zeros(unit.shape, F32) + count.astype(F32)
-    send_ref[...] = jnp.concatenate([embed, counts], axis=1).astype(BF16)
+    send = jnp.concatenate([embed, counts], axis=1).astype(BF16)
+    send_ref[...] = jnp.broadcast_to(send[None], send_ref.shape)
     pooled_ref[...] = pooled
     mixed_ref[...] = mixed_sum
     unit_ref[...] = unit
@@ -97,6 +98,7 @@
 def slope_kernel(
     send_ref, cut_ref, stem_ref, mix_ref, hidden_t_ref, patch_t_ref, stem_slope_ref, mix_slope_ref
 ):
+    del send_ref
     nodes = cut_ref.shape[0]
     voxels = stem_ref.shape[0]
     width = 2 * voxels
@@ -164,13 +166,13 @@
 
 
 def backward_kernel(
-    place_ref, gathered_ref, partner_ref, send_ref, pooled_ref, mixed_ref, unit_ref, inv_ref,
+    count_ref, gathered_ref, partner_ref, pooled_ref, mixed_ref, unit_ref, inv_ref,
     hidden_t_ref, patch_t_ref, stem_slope_ref, mix_slope_ref, mix_ref, out_ref, proj_ref, grad_ref,
 ):
     nodes, embed_dim = unit_ref.shape
     slots = gathered_ref.shape[0]
-    place = place_ref[0]
-    own_count = place_ref[1]
+    place = lax.axis_index("vol")
+    own_count = count_ref[...]
     channels = mix_ref.shape[0]
     voxels = patch_t_ref.shape[0] // 2
     blocks = stem_slope_ref.shape[0] // nodes
@@ -194,7 +196,8 @@
     companion = jnp.where(number_row == mate, 1.0, 0.0).astype(BF16)
 
     whole = gathered_ref[:, :embed_dim]
-    scores = nt(send_ref[:, :embed_dim], whole) / TEMPERATURE
+    own = gathered_ref[pl.ds(pl.multiple_of(place * nodes, nodes), nodes), :]
+    scores = nt(own[:, :embed_dim], whole) / TEMPERATURE
     other = jnp.logical_and(live_row, slot_row != rank + place * nodes)
     weight = jnp.where(other, jnp.exp(scores), 0.0)
     own_total = jnp.sum(weight, axis=1, keepdims=True)
@@ -208,8 +211,8 @@
     unit = unit_ref[...]
     radial = jnp.sum(unit * d_embed, axis=1, keepdims=True)
     d_raw = jnp.where(own_live, inv_ref[...] * (d_embed - unit * radial), 0.0).astype(BF16)
-    g_proj = tn(pooled_ref[...], d_raw)
-    d_sum = (nt(d_raw, proj_ref[...]) / (2 * blocks)).astype(BF16)
+    g_proj = tn(d_raw, pooled_ref[...])
+    d_sum = (nn(d_raw, proj_ref[...]) / (2 * blocks)).astype(BF16)
     high, low = split(mixed_ref[...])
     g_out = tn(high, d_sum) + tn(low, d_sum)
     d_mixed = nt(d_sum, out_ref[...])
@@ -246,17 +249,42 @@
         g_stem = g_stem + nn(patch_t_ref[:, rows], d_pre_stem)
     g_mix = g_mix[:channels, :channels] + g_mix[channels:, channels:]
     g_stem = g_stem[:voxels, :channels] + g_stem[voxels:, channels:]
-    half = channels // 2
-    g_proj = jnp.concatenate([g_proj[:half], g_proj[half:]], axis=1)
-    grad_ref[...] = jnp.concatenate([g_stem, g_mix, g_out, g_proj], axis=0).astype(grad_ref.dtype)
-
-
-def loss_kernel(place_ref, gathered_ref, partner_ref, anchor_ref, loss_ref, *, embed_dim, max_nodes):
+    pack(grad_ref, jnp.concatenate([g_stem, g_mix, g_out, g_proj], axis=0))
+
+
+def pack(ref, value):
+    if len(ref.shape) == 2:
+        ref[...] = value.astype(ref.dtype)
+        return
+    devices, share, width = ref.shape
+    full = share // 8 * 8
+    rest = share - full
+    head = value[: devices * full].reshape(devices, full, width)
+    ref[:, :full, :] = head.astype(ref.dtype)
+    if rest:
+        tail = value[devices * full :].reshape(devices, rest, width)
+        ref[:, full:, :] = tail.astype(ref.dtype)
+
+
+def unpack(ref):
+    if len(ref.shape) == 2:
+        return ref[...].astype(F32)
+    devices, share, width = ref.shape
+    full = share // 8 * 8
+    rest = share - full
+    value = ref[:, :full, :].astype(F32).reshape(devices * full, width)
+    if rest:
+        tail = ref[:, full:, :].astype(F32).reshape(devices * rest, width)
+        value = jnp.concatenate([value, tail], axis=0)
+    return value
+
+
+def loss_kernel(after_ref, gathered_ref, partner_ref, loss_ref, *, embed_dim, max_nodes):
+    del after_ref
     slots = gathered_ref.shape[0]
     owners = slots // max_nodes
-    place = place_ref[0]
-    node_dev = loss_ref.shape[0]
-    del anchor_ref
+    place = lax.axis_index("vol")
+    node_dev = loss_ref.shape[1]
     count_row, offset_row, _ = slot_tables(gathered_ref, embed_dim, max_nodes)
     slot_row = lax.broadcasted_iota(jnp.int32, (1, slots), 1)
     within = (slot_row % max_nodes).astype(F32)
@@ -273,63 +301,65 @@
     anchor = nn(jnp.where(mine, 1.0, 0.0).astype(BF16), whole)
     companion = nn(jnp.where(number_row == mate, 1.0, 0.0).astype(BF16), whole)
     positive = jnp.sum(anchor * companion, axis=1, keepdims=True) / TEMPERATURE
-    loss_ref[...] = jnp.broadcast_to(jnp.log(total) - positive, loss_ref.shape)
-
-
-def update_kernel(grad_ref, stem_ref, mix_ref, out_ref, proj_ref):
+    loss = jnp.log(total) - positive
+    row = lax.broadcasted_iota(jnp.int32, (node_dev, node_dev), 0)
+    column = lax.broadcasted_iota(jnp.int32, (node_dev, node_dev), 1)
+    loss_ref[...] = jnp.sum(jnp.where(row == column, loss, 0.0), axis=0, keepdims=True)
+
+
+def share_kernel(part_ref, send_ref):
+    total = jnp.sum(part_ref[...].astype(F32), axis=0, keepdims=True).astype(send_ref.dtype)
+    send_ref[...] = jnp.broadcast_to(total, send_ref.shape)
+
+
+def update_kernel(grad_ref, *refs):
+    value = unpack(grad_ref)
     start = 0
-    for ref in (stem_ref, mix_ref, out_ref, proj_ref):
-        size = ref.shape[0] * ref.shape[1]
-        rows = size // grad_ref.shape[1]
-        grad = grad_ref[start : start + rows, :].astype(F32)
+    for ref in refs:
+        rows = ref.shape[0]
+        grad = value[start : start + rows]
         start += rows
         squares = jnp.sum(jnp.sum(grad * grad, axis=0, keepdims=True), axis=1, keepdims=True)
-        update = grad * lax.rsqrt(squares / size + RMS_EPS)
-        if ref.shape[1] == grad_ref.shape[1]:
-            ref[...] = update
-        else:
-            half = ref.shape[1]
-            ref[:rows, :] = update[:, :half]
-            ref[rows:, :] = update[:, half:]
+        ref[...] = grad * lax.rsqrt(squares / (rows * ref.shape[1]) + RMS_EPS)
 
 
 def vmem(number):
     return [pl.BlockSpec(memory_space=pltpu.VMEM)] * number
 
 
-def smem():
-    return pl.BlockSpec(memory_space=pltpu.SMEM)
+def anywhere():
+    return pl.BlockSpec(memory_space=pl.ANY)
 
 
 def on_device(cutouts, counts, partner, w_stem, w_mix, w_out, w_proj):
     axes = ("vol", "rep")
     owners = lax.axis_size("vol")
     devices = owners * lax.axis_size("rep")
-    place = lax.axis_index("vol").astype(jnp.int32)
     cut = cutouts[0]
     nodes = cut.shape[0]
     voxels, channels = w_stem.shape
     embed_dim = w_proj.shape[1]
     rows = cut.shape[1] // (2 * voxels) * nodes
-    own_count = counts[0]
+    w_proj = w_proj.T
     shape = jax.ShapeDtypeStruct
+    params = pltpu.CompilerParams(vmem_limit_bytes=(16 << 20) + owners * nodes * 8192)
 
     send, pooled, mixed_sum, unit, inv = pl.pallas_call(
         forward_kernel,
         out_shape=(
-            shape((nodes, 2 * embed_dim), BF16),
+            shape((owners, nodes, 2 * embed_dim), BF16),
             shape((nodes, channels), BF16),
             shape((nodes, channels), F32),
             shape((nodes, embed_dim), F32),
             shape((nodes, 1), F32),
         ),
-        in_specs=[smem()] + vmem(5),
+        in_specs=vmem(6),
         out_specs=tuple(vmem(5)),
-    )(own_count, cut, w_stem, w_mix, w_out, w_proj)
-
-    gathered = lax.all_to_all(
-        jnp.broadcast_to(send[None], (owners,) + send.shape), "vol", 0, 0
-    ).reshape(owners * nodes, 2 * embed_dim)
+        compiler_params=params,
+        name="forward",
+    )(counts, cut, w_stem, w_mix, w_out, w_proj)
+
+    gathered = lax.all_to_all(send, "vol", 0, 0).reshape(owners * nodes, 2 * embed_dim)
 
     hidden_t, patch_t, stem_slope, mix_slope = pl.pallas_call(
         slope_kernel,
@@ -339,45 +369,64 @@
             shape((rows, 2 * channels), F32),
             shape((rows, 2 * channels), F32),
         ),
-        in_specs=vmem(4),
+        in_specs=[anywhere()] + vmem(3),
         out_specs=tuple(vmem(4)),
-    )(send, cut, w_stem, w_mix)
-
-    where = jnp.stack([place, own_count[0]])
-    total_rows = (w_stem.size + w_mix.size + w_out.size + w_proj.size) // channels
+        compiler_params=params,
+        name="slopes",
+    )(pooled, cut, w_stem, w_mix)
+
+    weights = (w_stem, w_mix, w_out, w_proj)
+    total_rows = sum(w.shape[0] for w in weights)
+    share = (total_rows + devices - 1) // devices
+    packed = share * devices == total_rows and share >= 8 and share % 4 == 0
     grad = pl.pallas_call(
         backward_kernel,
-        out_shape=shape((total_rows, channels), BF16),
-        in_specs=[smem()] + vmem(14),
+        out_shape=shape((devices, share, channels) if packed else (total_rows, channels), BF16),
+        in_specs=vmem(14),
         out_specs=vmem(1)[0],
+        compiler_params=params,
+        name="backward",
     )(
-        where, gathered, partner, send, pooled, mixed_sum, unit, inv,
+        counts, gathered, partner, pooled, mixed_sum, unit, inv,
         hidden_t, patch_t, stem_slope, mix_slope, w_mix, w_out, w_proj,
     )
 
-    share = (total_rows + devices - 1) // devices
-    if share * devices != total_rows:
-        grad = jnp.pad(grad, ((0, share * devices - total_rows), (0, 0)))
-    parts = lax.all_to_all(grad.reshape(devices, share, channels), axes, 0, 0)
-    mine = jnp.sum(parts.astype(F32), axis=0).astype(BF16)
-    whole = lax.all_to_all(jnp.broadcast_to(mine[None], (devices,) + mine.shape), axes, 0, 0)
-    whole = whole.reshape(devices * share, channels)[:total_rows]
+    parts = grad
+    if not packed:
+        parts = jnp.pad(grad, ((0, share * devices - total_rows), (0, 0)))
+        parts = parts.reshape(devices, share, channels)
+    parts = lax.all_to_all(parts, axes, 0, 0)
+    whole = pl.pallas_call(
+        share_kernel,
+        out_shape=shape(parts.shape, BF16),
+        in_specs=vmem(1),
+        out_specs=vmem(1)[0],
+        compiler_params=params,
+        name="share",
+    )(parts)
+    whole = lax.all_to_all(whole, axes, 0, 0)
+    if not packed:
+        whole = whole.reshape(devices * share, channels)[:total_rows]
 
     node_dev = partner.shape[1] // owners
     loss = pl.pallas_call(
         lambda *refs: loss_kernel(*refs, embed_dim=embed_dim, max_nodes=nodes),
-        out_shape=shape((node_dev, 128), F32),
-        in_specs=[smem()] + vmem(2) + [pl.BlockSpec(memory_space=pl.ANY)],
+        out_shape=shape((1, node_dev), F32),
+        in_specs=[anywhere()] + vmem(2),
         out_specs=vmem(1)[0],
-    )(where, gathered, partner, grad)
+        compiler_params=params,
+        name="losses",
+    )(grad, gathered, partner)
 
     updates = pl.pallas_call(
         update_kernel,
-        out_shape=tuple(shape(w.shape, F32) for w in (w_stem, w_mix, w_out, w_proj)),
+        out_shape=tuple(shape(w.shape, F32) for w in weights),
         in_specs=vmem(1),
         out_specs=tuple(vmem(4)),
+        compiler_params=params,
+        name="updates",
     )(whole)
-    return (*updates, loss[:, 0][None, None, :])
+    return (*updates[:3], updates[3].T, loss[None])
 
 
 def solution(mesh):

time: 53.5 us -> 46.5 us (0.87)
  Pallas kernels: 13.6 us -> 6.62 us
  waiting for transfers between devices: 8.14 us -> 13.3 us
  local copies, waits for them, and re-layouts: 8.49 us -> 4.57 us
  blocking collectives: 10.9 us -> 10.2 us
  other arithmetic: 0.63 us -> 0 us
    all_to_all x2, waiting for transfers between devices: 8.14 us -> 13.3 us  [the longest x1 7.2 us: on_device(): whole = lax.all_to_all(whole, axes, 0, 0)]
    pallas_call x2 -> x3, Pallas kernels: 6.81 us -> 4.03 us  [the longest x1 1.67 us: on_device(): pl.pallas_call(forward_kernel, out_shape=(shape((owners, nodes, 2 * embed...]
    pallas_call x1, Pallas kernels: 3.12 us -> 0.79 us  [on_device(): pl.pallas_call(slope_kernel, out_shape=(shape((2 * channels, rows), BF16)...]
    broadcast_in_dim x2 -> x0, local copies, waits for them, and re-layouts: 2 us -> none  [the longest x1 1.33 us: on_device(): jnp.broadcast_to(send[None], (owners,) + send.shape)]
    reshape x2 -> x0, local copies, waits for them, and re-layouts: 1.57 us -> none  [the longest x1 0.92 us: on_device(): parts = lax.all_to_all(grad.reshape(devices, share, channels), axes, 0, 0)]
    slice x1 -> x0, local copies, waits for them, and re-layouts: 1.32 us -> none  [on_device(): return (*updates, loss[:, 0][None, None, :])]
    unnamed x4 -> x22, local copies, waits for them, and re-layouts: 3.6 us -> 4.57 us
    pallas_call x1, Pallas kernels: 1.93 us -> 1 us  [on_device(): pl.pallas_call(lambda *refs: loss_kernel(*refs, embed_dim=embed_dim, max_...]
  transfers between devices with their start and end apart: 2 -> 2, of which waited for: 2 -> 2; matrix products, arithmetic and copies ran while one was open for 4% -> 0% of each run, Pallas kernels for 10% -> 4%
where the time goes in v2:
time: 46.5 us; the launch traced here: 45.9 us
  waiting for transfers between devices  13.3 us (29%)
  blocking collectives  10.2 us (22%)
  starting transfers between devices  9.98 us (21%)
  Pallas kernels  6.62 us (14%)
  local copies, waits for them, and re-layouts  4.57 us (10%)
  between operations  1.36 us (3%)
    all_to_all x1, blocking collectives, on_device(): parts = lax.all_to_all(parts, axes, 0, 0)  10.2 us
    all_to_all x1, starting transfers between devices, on_device(): lax.all_to_all(send, 'vol', 0, 0).reshape(owners * nodes, 2 * embed_dim)  7.41 us
    all_to_all x1, waiting for transfers between devices, on_device(): whole = lax.all_to_all(whole, axes, 0, 0)  7.2 us
    all_to_all x1, waiting for transfers between devices, on_device(): lax.all_to_all(send, 'vol', 0, 0).reshape(owners * nodes, 2 * embed_dim)  6.05 us
    unnamed x22, local copies, waits for them, and re-layouts  4.57 us
    all_to_all x1, starting transfers between devices, on_device(): whole = lax.all_to_all(whole, axes, 0, 0)  2.57 us
    pallas_call x1, Pallas kernels, on_device(): pl.pallas_call(forward_kernel, out_shape=(shape((owners, nodes, 2 * embed...  1.67 us
    pallas_call x1, Pallas kernels, on_device(): pl.pallas_call(backward_kernel, out_shape=shape((devices, share, channels...  1.65 us
  transfers between devices with their start and end apart: 2, of which 2 were waited for; matrix products, arithmetic and copies ran while one was open for 0% of the time, Pallas kernels for 4%

profile of v2, /device:TPU:0, one launch (start us, length us, event | category | flops | bytes accessed | tf_op | source)
XLA Modules:
  0.0 45.9 jit_solution(15261265461620932568)
XLA Ops:
  1.3 0.0 copy-start
  1.3 0.9 %copy-done = bf16[1,32,4096]{2,1,0:T(8,128)(2,1)S(1)} copy-done((bf16[1,32,4096]{2,1,0:T(8,128)(2,1)S(1)}, bf16[1,32,4096]{2,1,0:T(8,128)(2,1)}, u32[]{:S(2)}) %copy-start) | copy-done | bytes 262168
  2.2 0.0 copy-start.2
  2.2 0.8 %copy-done.2 = bf16[128,128]{1,0:T(8,128)(2,1)S(1)} copy-done((bf16[128,128]{1,0:T(8,128)(2,1)S(1)}, bf16[128,128]{1,0:T(8,128)(2,1)}, u32[]{:S(2)}) %copy-start.2) | copy-done | bytes 32792
  3.0 0.0 copy-start.4
  3.0 0.8 %copy-done.4 = bf16[128,128]{1,0:T(8,128)(2,1)S(1)} copy-done((bf16[128,128]{1,0:T(8,128)(2,1)S(1)}, bf16[128,128]{1,0:T(8,128)(2,1)}, u32[]{:S(2)}) %copy-start.4) | copy-done | bytes 32792
  3.7 0.0 copy-start.6
  3.7 0.7 %copy-done.6 = bf16[128,64]{0,1:T(8,128)(2,1)S(1)} copy-done((bf16[128,64]{0,1:T(8,128)(2,1)S(1)}, bf16[128,64]{0,1:T(8,128)(2,1)}, u32[]{:S(2)}) %copy-start.6) | copy-done | bytes 16408
  4.5 0.0 copy-start.8
  4.5 0.7 %copy-done.8 = bf16[64,128]{1,0:T(8,128)(2,1)S(1)} copy-done((bf16[64,128]{1,0:T(8,128)(2,1)S(1)}, bf16[64,128]{1,0:T(8,128)(2,1)}, u32[]{:S(2)}) %copy-start.8) | copy-done | bytes 16408
  5.2 0.0 copy-start.1
  5.2 1.7 %forward.1 = (bf16[8,32,128]{2,1,0:T(8,128)(2,1)}, bf16[32,128]{1,0:T(8,128)(2,1)S(1)}, f32[32,128]{1,0:T(8,128)S(1)}, f32[32,64]{1,0:T(8,128)S(1)}, f32[32,1]{1,0:T(8,128)S(1)}) custom-call(s32[1,1]{1,0:T(1,128)S(6)} %copy.12.count_ref, bf16[32,4096]{1,0:T(8,128)(2,1)S(1)} %bitcast.5, bf16[64,128]{1,0:T(8,128)(2,1)S(1)} %copy-done.8, ...), custom_call_target="tpu_custom_call" | custom-call | tf_op jit(solution)/shard_map/forward/pallas_call | solution.py:347
  6.9 0.0 copy-start.3
  6.9 0.0 copy-start.9
  6.9 7.4 %all-to-all-start = ((bf16[8,32,128]{2,1,0:T(8,128)(2,1)}), bf16[8,32,128]{2,1,0:T(8,128)(2,1)S(1)}, u32[]{:S(2)}, u32[]{:S(2)}) async-start(bf16[8,32,128]{2,1,0:T(8,128)(2,1)} %get-tuple-element.18), calls=%async_computation | async-start | bytes 131072 | tf_op jit(solution)/shard_map/all_to_all | solution.py:362
  14.3 0.0 copy-done.1
  14.3 0.0 copy-done.3
  14.3 0.0 copy-done.9
  14.3 0.0 copy-start.5
  14.3 0.0 copy-start.7
  14.3 0.8 %slopes.1 = (bf16[256,1024]{1,0:T(8,128)(2,1)S(1)}, bf16[128,1024]{1,0:T(8,128)(2,1)S(1)}, f32[1024,256]{1,0:T(8,128)S(1)}, f32[1024,256]{1,0:T(8,128)S(1)}) custom-call(bf16[32,128]{1,0:T(8,128)(2,1)S(1)} %get-tuple-element.19.send_ref.pooled_ref, bf16[32,4096]{1,0:T(8,128)(2,1)S(1)} %bitcast.6, bf16[64,128]{1,0:T(8,128)(2,1)S(1)} %copy-done.9, ...), custom_call_target="tpu_custom_call" | custom-call | tf_op jit(solution)/shard_map/slopes/pallas_call | solution.py:364
  15.1 6.1 %all-to-all-done = bf16[8,32,128]{2,1,0:T(8,128)(2,1)S(1)} async-done(((bf16[8,32,128]{2,1,0:T(8,128)(2,1)}), bf16[8,32,128]{2,1,0:T(8,128)(2,1)S(1)}, u32[]{:S(2)}, u32[]{:S(2)}) %all-to-all-start) | async-done | bytes 65568 | tf_op jit(solution)/shard_map/all_to_all | solution.py:362
  21.2 0.0 copy-start.10
  21.2 0.0 copy-done.5
  21.2 0.0 copy-done.7
  21.2 0.6 %copy-done.10 = s32[1,128]{1,0:T(1,128)S(1)} copy-done((s32[1,128]{1,0:T(1,128)S(1)}, s32[1,128]{1,0:T(1,128)}, u32[]{:S(2)}) %copy-start.10) | copy-done | bytes 536
  21.8 1.7 %backward.1.refs_0_ = bf16[32,12,128]{2,1,0:T(8,128)(2,1)S(1)} custom-call(s32[1,1]{1,0:T(1,128)S(6)} %copy.12.count_ref, bf16[256,128]{1,0:T(8,128)(2,1)S(1)} %bitcast.7, s32[1,128]{1,0:T(1,128)S(1)} %copy-done.10, bf16[32,128]{1,0:T(8,128)(2,1)S(1)} %get-tuple-element.19.send_ref.pooled_ref, f32[32,128]{1,0:T(8,128)S(1)} %get-tuple-element.20.mixed_ref, ...), custom_call_target="tpu_custom_call" | custom-call | tf_op jit(solution)/shard_map/backward/pallas_call | solution.py:382
  23.5 10.2 %all_to_all.15.part_ref = bf16[32,12,128]{2,1,0:T(8,128)(2,1)S(1)} all-to-all(bf16[32,12,128]{2,1,0:T(8,128)(2,1)S(1)} %backward.1.refs_0_), channel_id=1, replica_groups=mesh['vol'=8,'rep'=4] {'vol','rep'}, dimensions={0} | all-to-all | bytes 196608 | tf_op jit(solution)/shard_map/all_to_all | solution.py:398
  33.7 0.7 %share.1 = bf16[32,12,128]{2,1,0:T(8,128)(2,1)} custom-call(bf16[32,12,128]{2,1,0:T(8,128)(2,1)S(1)} %all_to_all.15.part_ref), custom_call_target="tpu_custom_call" | custom-call | tf_op jit(solution)/shard_map/share/pallas_call | solution.py:399
  34.4 2.6 %all-to-all-start.2 = ((bf16[32,12,128]{2,1,0:T(8,128)(2,1)}), bf16[32,12,128]{2,1,0:T(8,128)(2,1)S(1)}, u32[]{:S(2)}, u32[]{:S(2)}) async-start(bf16[32,12,128]{2,1,0:T(8,128)(2,1)} %share.1), calls=%async_computation.2 | async-start | bytes 262144 | tf_op jit(solution)/shard_map/all_to_all | solution.py:407
  36.9 1.0 %losses.1 = f32[1,16]{1,0:T(1,128)} custom-call(bf16[32,12,128]{2,1,0:T(8,128)(2,1)S(1)} %backward.1.refs_0_, bf16[256,128]{1,0:T(8,128)(2,1)S(1)} %bitcast.8, s32[1,128]{1,0:T(1,128)S(1)} %copy-done.10), custom_call_target="tpu_custom_call" | custom-call | tf_op jit(solution)/shard_map/losses/pallas_call | solution.py:412
  37.9 7.2 %all-to-all-done.2.grad_ref = bf16[32,12,128]{2,1,0:T(8,128)(2,1)S(1)} async-done(((bf16[32,12,128]{2,1,0:T(8,128)(2,1)}), bf16[32,12,128]{2,1,0:T(8,128)(2,1)S(1)}, u32[]{:S(2)}, u32[]{:S(2)}) %all-to-all-start.2) | async-done | bytes 98336 | tf_op jit(solution)/shard_map/all_to_all | solution.py:407
  45.1 0.8 %updates.1 = (f32[64,128]{1,0:T(8,128)}, f32[128,128]{1,0:T(8,128)}, f32[128,128]{1,0:T(8,128)}, f32[64,128]{1,0:T(8,128)}) custom-call(bf16[32,12,128]{2,1,0:T(8,128)(2,1)S(1)} %all-to-all-done.2.grad_ref), custom_call_target="tpu_custom_call" | custom-call | tf_op jit(solution)/shard_map/updates/pallas_call | solution.py:421
Async XLA Ops:
  1.3 1.0 %copy-start = (bf16[1,32,4096]{2,1,0:T(8,128)(2,1)S(1)}, bf16[1,32,4096]{2,1,0:T(8,128)(2,1)}, u32[]{:S(2)}) copy-start(bf16[1,32,4096]{2,1,0:T(8,128)(2,1)} %param.7) | copy-start | bytes 786436
  2.2 0.8 %copy-start.2 = (bf16[128,128]{1,0:T(8,128)(2,1)S(1)}, bf16[128,128]{1,0:T(8,128)(2,1)}, u32[]{:S(2)}) copy-start(bf16[128,128]{1,0:T(8,128)(2,1)} %mix_ref.5) | copy-start | bytes 98308
  3.0 0.8 %copy-start.4 = (bf16[128,128]{1,0:T(8,128)(2,1)S(1)}, bf16[128,128]{1,0:T(8,128)(2,1)}, u32[]{:S(2)}) copy-start(bf16[128,128]{1,0:T(8,128)(2,1)} %out_ref.3) | copy-start | bytes 98308
  3.7 0.7 %copy-start.6 = (bf16[128,64]{0,1:T(8,128)(2,1)S(1)}, bf16[128,64]{0,1:T(8,128)(2,1)}, u32[]{:S(2)}) copy-start(bf16[128,64]{0,1:T(8,128)(2,1)} %param.13) | copy-start | bytes 49156
  4.5 0.7 %copy-start.8 = (bf16[64,128]{1,0:T(8,128)(2,1)S(1)}, bf16[64,128]{1,0:T(8,128)(2,1)}, u32[]{:S(2)}) copy-start(bf16[64,128]{1,0:T(8,128)(2,1)} %stem_ref.3) | copy-start | bytes 49156
  5.2 9.1 %copy-start.1 = (bf16[1,32,4096]{2,1,0:T(8,128)(2,1)S(1)}, bf16[1,32,4096]{2,1,0:T(8,128)(2,1)}, u32[]{:S(2)}) copy-start(bf16[1,32,4096]{2,1,0:T(8,128)(2,1)} %param.7) | copy-start | bytes 786436
  6.9 7.4 %copy-start.3 = (bf16[128,128]{1,0:T(8,128)(2,1)S(1)}, bf16[128,128]{1,0:T(8,128)(2,1)}, u32[]{:S(2)}) copy-start(bf16[128,128]{1,0:T(8,128)(2,1)} %mix_ref.5) | copy-start | bytes 98308
  6.9 7.4 %copy-start.9 = (bf16[64,128]{1,0:T(8,128)(2,1)S(1)}, bf16[64,128]{1,0:T(8,128)(2,1)}, u32[]{:S(2)}) copy-start(bf16[64,128]{1,0:T(8,128)(2,1)} %stem_ref.3) | copy-start | bytes 49156
  6.9 14.3 %all-to-all-start = ((bf16[8,32,128]{2,1,0:T(8,128)(2,1)}), bf16[8,32,128]{2,1,0:T(8,128)(2,1)S(1)}, u32[]{:S(2)}, u32[]{:S(2)}) async-start(bf16[8,32,128]{2,1,0:T(8,128)(2,1)} %get-tuple-element.18), calls=%async_computation | async-start | bytes 131072 | tf_op jit(solution)/shard_map/all_to_all | solution.py:362
  14.3 6.9 %copy-start.5 = (bf16[128,128]{1,0:T(8,128)(2,1)S(1)}, bf16[128,128]{1,0:T(8,128)(2,1)}, u32[]{:S(2)}) copy-start(bf16[128,128]{1,0:T(8,128)(2,1)} %out_ref.3) | copy-start | bytes 98308
  14.3 6.9 %copy-start.7 = (bf16[128,64]{0,1:T(8,128)(2,1)S(1)}, bf16[128,64]{0,1:T(8,128)(2,1)}, u32[]{:S(2)}) copy-start(bf16[128,64]{0,1:T(8,128)(2,1)} %param.13) | copy-start | bytes 49156
  21.2 0.7 %copy-start.10 = (s32[1,128]{1,0:T(1,128)S(1)}, s32[1,128]{1,0:T(1,128)}, u32[]{:S(2)}) copy-start(s32[1,128]{1,0:T(1,128)} %refs_2_.1) | copy-start | bytes 1540
  34.4 10.8 %all-to-all-start.2 = ((bf16[32,12,128]{2,1,0:T(8,128)(2,1)}), bf16[32,12,128]{2,1,0:T(8,128)(2,1)S(1)}, u32[]{:S(2)}, u32[]{:S(2)}) async-start(bf16[32,12,128]{2,1,0:T(8,128)(2,1)} %share.1), calls=%async_computation.2 | async-start | bytes 262144 | tf_op jit(solution)/shard_map/all_to_all | solution.py:407

commit v3 on v2

--- a/solution.py
+++ b/solution.py
@@ -53,21 +53,47 @@
 
 
 def forward_kernel(
-    count_ref, cut_ref, stem_ref, mix_ref, out_ref, proj_ref,
+    count_ref, cut_hbm, stem_hbm, mix_hbm, out_hbm, proj_hbm,
     send_ref, pooled_ref, mixed_ref, unit_ref, inv_ref,
+    cut_ref, stem_ref, mix_ref, out_ref, proj_ref, sems, cut_sems,
 ):
     nodes = cut_ref.shape[0]
     voxels, channels = stem_ref.shape
     width = 2 * voxels
     blocks = cut_ref.shape[1] // width
+
+    def cut_copy(first):
+        lanes = pl.ds(first * width, min(GROUP, blocks - first) * width)
+        return pltpu.make_async_copy(
+            cut_hbm.at[:, lanes], cut_ref.at[:, lanes], cut_sems.at[first // GROUP]
+        )
+
+    def copy(index, source, target):
+        return pltpu.make_async_copy(source, target, sems.at[index])
+
+    stem_copy = copy(0, stem_hbm, stem_ref)
+    mix_copy = copy(1, mix_hbm, mix_ref)
+    late = (copy(2, out_hbm, out_ref), copy(3, proj_hbm, proj_ref))
+    stem_copy.start()
+    cut_copy(0).start()
+    mix_copy.start()
+    for first in range(GROUP, blocks, GROUP):
+        cut_copy(first).start()
+    for each in late:
+        each.start()
+    stem_copy.wait()
     stem2 = paired(stem_ref[...])
-    mix2 = paired(mix_ref[...])
+    mix2 = None
     hidden_sum = jnp.zeros((nodes, 2 * channels), F32)
     mixed_sum = jnp.zeros((nodes, 2 * channels), F32)
     for first in range(0, blocks, GROUP):
         number = min(GROUP, blocks - first)
+        cut_copy(first).wait()
         pre_stem = nn(pair_rows(cut_ref, width, first, number), stem2)
         hidden = (pre_stem * sigmoid(pre_stem)).astype(BF16)
+        if first == 0:
+            mix_copy.wait()
+            mix2 = paired(mix_ref[...])
         pre_mix = nn(hidden, mix2)
         mixed = (pre_mix * sigmoid(pre_mix)).astype(BF16)
         for i in range(number):
@@ -77,13 +103,15 @@
     hidden_sum = hidden_sum[:, :channels] + hidden_sum[:, channels:]
     mixed_sum = mixed_sum[:, :channels] + mixed_sum[:, channels:]
     high, low = split(mixed_sum)
+    for each in late:
+        each.wait()
     weight = out_ref[...]
     summed = hidden_sum + (nn(high, weight) + nn(low, weight))
     pooled = (summed / (2 * blocks)).astype(BF16)
     raw = nt(pooled, proj_ref[...])
     inv = lax.rsqrt(jnp.sum(raw * raw, axis=1, keepdims=True) + NORM_EPS)
     unit = raw * inv
-    count = count_ref[...]
+    count = count_ref[0, 0]
     live = lax.broadcasted_iota(jnp.int32, unit.shape, 0) < count
     embed = jnp.where(live, unit, 0.0)
     counts = jnp.zeros(unit.shape, F32) + count.astype(F32)
@@ -96,9 +124,11 @@
 
 
 def slope_kernel(
-    send_ref, cut_ref, stem_ref, mix_ref, hidden_t_ref, patch_t_ref, stem_slope_ref, mix_slope_ref
+    after_ref, cut_ref, stem_ref, mix_ref, partner_ref,
+    hidden_t_ref, patch_t_ref, stem_slope_ref, mix_slope_ref, mate_ref,
 ):
-    del send_ref
+    del after_ref
+    mate_ref[...] = partner_ref[...].astype(F32)
     nodes = cut_ref.shape[0]
     voxels = stem_ref.shape[0]
     width = 2 * voxels
@@ -165,14 +195,19 @@
     return jnp.where(live_row, total, 1.0)
 
 
+def look_up(table_ref, number):
+    shape = (number.shape[0], table_ref.shape[1])
+    listed = lax.broadcasted_iota(jnp.int32, shape, 1).astype(F32)
+    return jnp.sum(jnp.where(listed == number, table_ref[...], 0.0), axis=1, keepdims=True)
+
+
 def backward_kernel(
-    count_ref, gathered_ref, partner_ref, pooled_ref, mixed_ref, unit_ref, inv_ref,
-    hidden_t_ref, patch_t_ref, stem_slope_ref, mix_slope_ref, mix_ref, out_ref, proj_ref, grad_ref,
+    gathered_ref, mate_ref, pooled_ref, mixed_ref, unit_ref, inv_ref,
+    hidden_t_ref, patch_t_ref, stem_slope_ref, mix_slope_ref, mix_ref, out_ref, proj_ref, grad_ref, loss_ref,
 ):
     nodes, embed_dim = unit_ref.shape
     slots = gathered_ref.shape[0]
     place = lax.axis_index("vol")
-    own_count = count_ref[...]
     channels = mix_ref.shape[0]
     voxels = patch_t_ref.shape[0] // 2
     blocks = stem_slope_ref.shape[0] // nodes
@@ -188,15 +223,13 @@
         jnp.where(slot_row // nodes < place, heads, 0.0), axis=1, keepdims=True
     )
     rank = lax.broadcasted_iota(jnp.int32, (nodes, 1), 0)
-    own_live = rank < own_count
     own_number = own_offset + rank.astype(F32)
-    partner = partner_ref[...].astype(F32)
-    listed = lax.broadcasted_iota(jnp.int32, (nodes, partner.shape[1]), 1).astype(F32)
-    mate = jnp.sum(jnp.where(listed == own_number, partner, 0.0), axis=1, keepdims=True)
+    mate = look_up(mate_ref, own_number)
     companion = jnp.where(number_row == mate, 1.0, 0.0).astype(BF16)
 
     whole = gathered_ref[:, :embed_dim]
     own = gathered_ref[pl.ds(pl.multiple_of(place * nodes, nodes), nodes), :]
+    own_live = rank.astype(F32) < own[:, embed_dim : embed_dim + 1].astype(F32)
     scores = nt(own[:, :embed_dim], whole) / TEMPERATURE
     other = jnp.logical_and(live_row, slot_row != rank + place * nodes)
     weight = jnp.where(other, jnp.exp(scores), 0.0)
@@ -207,6 +240,19 @@
     d_embed = (
         mixed_rows[:nodes] + mixed_rows[nodes : 2 * nodes] - 2.0 * mixed_rows[2 * nodes :]
     ) / TEMPERATURE
+
+    node_dev = loss_ref.shape[1]
+    owners = slots // nodes
+    wanted = (lax.broadcasted_iota(jnp.int32, (node_dev, 1), 0) * owners + place).astype(F32)
+    mine = number_row == wanted
+    total = jnp.sum(jnp.where(mine, totals, 0.0), axis=1, keepdims=True)
+    anchor = nn(jnp.where(mine, 1.0, 0.0).astype(BF16), whole)
+    other_end = number_row == look_up(mate_ref, wanted)
+    other_end = nn(jnp.where(other_end, 1.0, 0.0).astype(BF16), whole)
+    loss = jnp.log(total) - jnp.sum(anchor * other_end, axis=1, keepdims=True) / TEMPERATURE
+    row = lax.broadcasted_iota(jnp.int32, (node_dev, node_dev), 0)
+    column = lax.broadcasted_iota(jnp.int32, (node_dev, node_dev), 1)
+    loss_ref[...] = jnp.sum(jnp.where(row == column, loss, 0.0), axis=0, keepdims=True)
 
     unit = unit_ref[...]
     radial = jnp.sum(unit * d_embed, axis=1, keepdims=True)
@@ -249,71 +295,19 @@
         g_stem = g_stem + nn(patch_t_ref[:, rows], d_pre_stem)
     g_mix = g_mix[:channels, :channels] + g_mix[channels:, channels:]
     g_stem = g_stem[:voxels, :channels] + g_stem[voxels:, channels:]
-    pack(grad_ref, jnp.concatenate([g_stem, g_mix, g_out, g_proj], axis=0))
-
-
-def pack(ref, value):
-    if len(ref.shape) == 2:
-        ref[...] = value.astype(ref.dtype)
-        return
-    devices, share, width = ref.shape
-    full = share // 8 * 8
-    rest = share - full
-    head = value[: devices * full].reshape(devices, full, width)
-    ref[:, :full, :] = head.astype(ref.dtype)
-    if rest:
-        tail = value[devices * full :].reshape(devices, rest, width)
-        ref[:, full:, :] = tail.astype(ref.dtype)
-
-
-def unpack(ref):
-    if len(ref.shape) == 2:
-        return ref[...].astype(F32)
-    devices, share, width = ref.shape
-    full = share // 8 * 8
-    rest = share - full
-    value = ref[:, :full, :].astype(F32).reshape(devices * full, width)
-    if rest:
-        tail = ref[:, full:, :].astype(F32).reshape(devices * rest, width)
-        value = jnp.concatenate([value, tail], axis=0)
-    return value
-
-
-def loss_kernel(after_ref, gathered_ref, partner_ref, loss_ref, *, embed_dim, max_nodes):
-    del after_ref
-    slots = gathered_ref.shape[0]
-    owners = slots // max_nodes
-    place = lax.axis_index("vol")
-    node_dev = loss_ref.shape[1]
-    count_row, offset_row, _ = slot_tables(gathered_ref, embed_dim, max_nodes)
-    slot_row = lax.broadcasted_iota(jnp.int32, (1, slots), 1)
-    within = (slot_row % max_nodes).astype(F32)
-    live_row = within < count_row
-    number_row = jnp.where(live_row, offset_row + within, -1.0)
-    totals = score_sums(gathered_ref, embed_dim, max_nodes, live_row)
-    number = (lax.broadcasted_iota(jnp.int32, (node_dev, 1), 0) * owners + place).astype(F32)
-    partner = partner_ref[...].astype(F32)
-    listed = lax.broadcasted_iota(jnp.int32, (node_dev, partner.shape[1]), 1).astype(F32)
-    mate = jnp.sum(jnp.where(listed == number, partner, 0.0), axis=1, keepdims=True)
-    mine = number_row == number
-    total = jnp.sum(jnp.where(mine, totals, 0.0), axis=1, keepdims=True)
-    whole = gathered_ref[:, :embed_dim]
-    anchor = nn(jnp.where(mine, 1.0, 0.0).astype(BF16), whole)
-    companion = nn(jnp.where(number_row == mate, 1.0, 0.0).astype(BF16), whole)
-    positive = jnp.sum(anchor * companion, axis=1, keepdims=True) / TEMPERATURE
-    loss = jnp.log(total) - positive
-    row = lax.broadcasted_iota(jnp.int32, (node_dev, node_dev), 0)
-    column = lax.broadcasted_iota(jnp.int32, (node_dev, node_dev), 1)
-    loss_ref[...] = jnp.sum(jnp.where(row == column, loss, 0.0), axis=0, keepdims=True)
-
-
-def share_kernel(part_ref, send_ref):
-    total = jnp.sum(part_ref[...].astype(F32), axis=0, keepdims=True).astype(send_ref.dtype)
-    send_ref[...] = jnp.broadcast_to(total, send_ref.shape)
+    grads = jnp.concatenate([g_stem, g_mix, g_out, g_proj], axis=0)
+    grad_ref[...] = grads.reshape(grad_ref.shape).astype(grad_ref.dtype)
+
+
+def share_kernel(part_ref, send_ref, *, devices):
+    parts = part_ref[...].astype(F32)
+    total = jnp.sum(parts.reshape((devices, -1) + parts.shape[1:]), axis=0, keepdims=True)
+    total = jnp.broadcast_to(total.astype(send_ref.dtype), (devices,) + total.shape[1:])
+    send_ref[...] = total.reshape(send_ref.shape)
 
 
 def update_kernel(grad_ref, *refs):
-    value = unpack(grad_ref)
+    value = grad_ref[...].astype(F32).reshape(-1, grad_ref.shape[-1])
     start = 0
     for ref in refs:
         rows = ref.shape[0]
@@ -327,8 +321,12 @@
     return [pl.BlockSpec(memory_space=pltpu.VMEM)] * number
 
 
-def anywhere():
-    return pl.BlockSpec(memory_space=pl.ANY)
+def anywhere(number):
+    return [pl.BlockSpec(memory_space=pl.ANY)] * number
+
+
+def hbm(number):
+    return [pl.BlockSpec(memory_space=pltpu.HBM)] * number
 
 
 def on_device(cutouts, counts, partner, w_stem, w_mix, w_out, w_proj):
@@ -340,7 +338,9 @@
     voxels, channels = w_stem.shape
     embed_dim = w_proj.shape[1]
     rows = cut.shape[1] // (2 * voxels) * nodes
+    groups = (cut.shape[1] // (2 * voxels) + GROUP - 1) // GROUP
     w_proj = w_proj.T
+    weights = (w_stem, w_mix, w_out, w_proj)
     shape = jax.ShapeDtypeStruct
     params = pltpu.CompilerParams(vmem_limit_bytes=(16 << 20) + owners * nodes * 8192)
 
@@ -353,70 +353,63 @@
             shape((nodes, embed_dim), F32),
             shape((nodes, 1), F32),
         ),
-        in_specs=vmem(6),
+        in_specs=[pl.BlockSpec(memory_space=pltpu.SMEM)] + hbm(5),
         out_specs=tuple(vmem(5)),
+        scratch_shapes=[pltpu.VMEM(a.shape, BF16) for a in (cut,) + weights]
+        + [pltpu.SemaphoreType.DMA((4,)), pltpu.SemaphoreType.DMA((groups,))],
         compiler_params=params,
         name="forward",
-    )(counts, cut, w_stem, w_mix, w_out, w_proj)
+    )(counts, *(pltpu.with_memory_space_constraint(a, pltpu.HBM) for a in (cut, *weights)))
 
     gathered = lax.all_to_all(send, "vol", 0, 0).reshape(owners * nodes, 2 * embed_dim)
 
-    hidden_t, patch_t, stem_slope, mix_slope = pl.pallas_call(
+    hidden_t, patch_t, stem_slope, mix_slope, mates = pl.pallas_call(
         slope_kernel,
         out_shape=(
             shape((2 * channels, rows), BF16),
             shape((2 * voxels, rows), BF16),
             shape((rows, 2 * channels), F32),
             shape((rows, 2 * channels), F32),
+            shape(partner.shape, F32),
         ),
-        in_specs=[anywhere()] + vmem(3),
-        out_specs=tuple(vmem(4)),
+        in_specs=anywhere(1) + vmem(4),
+        out_specs=tuple(vmem(5)),
         compiler_params=params,
         name="slopes",
-    )(pooled, cut, w_stem, w_mix)
-
-    weights = (w_stem, w_mix, w_out, w_proj)
+    )(pooled, cut, w_stem, w_mix, partner)
+
     total_rows = sum(w.shape[0] for w in weights)
     share = (total_rows + devices - 1) // devices
-    packed = share * devices == total_rows and share >= 8 and share % 4 == 0
-    grad = pl.pallas_call(
+    tile = next(t for t in (8, 4, 2, 1) if share % t == 0)
+    padded = share * devices - total_rows
+    parts, loss = pl.pallas_call(
         backward_kernel,
-        out_shape=shape((devices, share, channels) if packed else (total_rows, channels), BF16),
-        in_specs=vmem(14),
-        out_specs=vmem(1)[0],
+        out_shape=(
+            shape((total_rows, channels) if padded else (total_rows // tile, tile, channels), BF16),
+            shape((1, partner.shape[1] // owners), F32),
+        ),
+        in_specs=vmem(13),
+        out_specs=tuple(vmem(2)),
         compiler_params=params,
         name="backward",
     )(
-        counts, gathered, partner, pooled, mixed_sum, unit, inv,
+        gathered, mates, pooled, mixed_sum, unit, inv,
         hidden_t, patch_t, stem_slope, mix_slope, w_mix, w_out, w_proj,
     )
-
-    parts = grad
-    if not packed:
-        parts = jnp.pad(grad, ((0, share * devices - total_rows), (0, 0)))
-        parts = parts.reshape(devices, share, channels)
-    parts = lax.all_to_all(parts, axes, 0, 0)
+    if padded:
+        parts = jnp.pad(parts, ((0, padded), (0, 0))).reshape(-1, tile, channels)
+    parts = lax.all_to_all(parts, axes, 0, 0, tiled=True)
     whole = pl.pallas_call(
-        share_kernel,
+        lambda *refs: share_kernel(*refs, devices=devices),
         out_shape=shape(parts.shape, BF16),
         in_specs=vmem(1),
         out_specs=vmem(1)[0],
         compiler_params=params,
         name="share",
     )(parts)
-    whole = lax.all_to_all(whole, axes, 0, 0)
-    if not packed:
-        whole = whole.reshape(devices * share, channels)[:total_rows]
-
-    node_dev = partner.shape[1] // owners
-    loss = pl.pallas_call(
-        lambda *refs: loss_kernel(*refs, embed_dim=embed_dim, max_nodes=nodes),
-        out_shape=shape((1, node_dev), F32),
-        in_specs=[anywhere()] + vmem(2),
-        out_specs=vmem(1)[0],
-        compiler_params=params,
-        name="losses",
-    )(grad, gathered, partner)
+    whole = lax.all_to_all(whole, axes, 0, 0, tiled=True)
+    if padded:
+        whole = whole.reshape(-1, channels)[:total_rows]
 
     updates = pl.pallas_call(
         update_kernel,

time: 46.5 us -> 42.4 us (0.912)
  blocking collectives: 10.2 us -> 19.2 us
  waiting for transfers between devices: 13.3 us -> 5.44 us
  local copies, waits for them, and re-layouts: 4.57 us -> 0.65 us
  starting transfers between devices: 9.98 us -> 7.29 us
  Pallas kernels: 6.62 us -> 8.06 us
    all_to_all x1 -> x2, blocking collectives: 10.2 us -> 19.2 us  [the longest x1 9.73 us: on_device(): parts = lax.all_to_all(parts, axes, 0, 0, tiled=True)]
    all_to_all x1 -> x0, waiting for transfers between devices: 7.2 us -> none  [on_device(): whole = lax.all_to_all(whole, axes, 0, 0)]
    unnamed x22 -> x12, local copies, waits for them, and re-layouts: 4.57 us -> 0.65 us
    pallas_call x1, Pallas kernels: 1.67 us -> 4.41 us  [on_device(): pl.pallas_call(forward_kernel, out_shape=(shape((owners, nodes, 2 * embed...]
    all_to_all x1 -> x0, starting transfers between devices: 2.57 us -> none  [on_device(): whole = lax.all_to_all(whole, axes, 0, 0)]
    pallas_call x3 -> x2, Pallas kernels: 3.36 us -> 2.05 us  [the longest x1 1.98 us: on_device(): pl.pallas_call(backward_kernel, out_shape=(shape((total_rows, channels) i...]
    all_to_all x1, waiting for transfers between devices: 6.05 us -> 5.44 us  [on_device(): lax.all_to_all(send, 'vol', 0, 0).reshape(owners * nodes, 2 * embed_dim)]
  transfers between devices with their start and end apart: 2 -> 1, of which waited for: 2 -> 1; matrix products, arithmetic and copies ran while one was open for 0% -> 0% of each run, Pallas kernels for 4% -> 2%
where the time goes in v3:
time: 42.4 us; the launch traced here: 42 us
  blocking collectives  19.2 us (45%)
  Pallas kernels  8.06 us (19%)
  starting transfers between devices  7.29 us (17%)
  waiting for transfers between devices  5.44 us (13%)
  between operations  1.4 us (3%)
  local copies, waits for them, and re-layouts  0.65 us (2%)
    all_to_all x1, blocking collectives, on_device(): parts = lax.all_to_all(parts, axes, 0, 0, tiled=True)  9.73 us
    all_to_all x1, blocking collectives, on_device(): whole = lax.all_to_all(whole, axes, 0, 0, tiled=True)  9.48 us
    all_to_all x1, starting transfers between devices, on_device(): lax.all_to_all(send, 'vol', 0, 0).reshape(owners * nodes, 2 * embed_dim)  7.29 us
    all_to_all x1, waiting for transfers between devices, on_device(): lax.all_to_all(send, 'vol', 0, 0).reshape(owners * nodes, 2 * embed_dim)  5.44 us
    pallas_call x1, Pallas kernels, on_device(): pl.pallas_call(forward_kernel, out_shape=(shape((owners, nodes, 2 * embed...  4.41 us
    pallas_call x1, Pallas kernels, on_device(): pl.pallas_call(backward_kernel, out_shape=(shape((total_rows, channels) i...  1.98 us
  transfers between devices with their start and end apart: 1, of which 1 were waited for; matrix products, arithmetic and copies ran while one was open for 0% of the time, Pallas kernels for 2%

profile of v3, /device:TPU:0, one launch (start us, length us, event | category | flops | bytes accessed | tf_op | source)
XLA Modules:
  0.0 42.0 jit_solution(891891945639110093)
XLA Ops:
  0.6 0.0 copy-start
  1.3 4.4 %forward.1 = (bf16[8,32,128]{2,1,0:T(8,128)(2,1)}, bf16[32,128]{1,0:T(8,128)(2,1)S(1)}, f32[32,128]{1,0:T(8,128)S(1)}, f32[32,64]{1,0:T(8,128)S(1)}, f32[32,1]{1,0:T(8,128)S(1)}) custom-call(s32[1,1]{1,0:T(1,128)S(6)} %copy.12.count_ref, bf16[32,4096]{1,0:T(8,128)(2,1)} %bitcast.5, bf16[64,128]{1,0:T(8,128)(2,1)} %stem_ref.1, bf16[128,128]{1,0:T(8,128)(2,1)} %mix_ref.3, ...), custom_call_target="tpu_custom_call" | custom-call | tf_op jit(solution)/shard_map/forward/pallas_call | solution.py:347
  5.7 0.0 copy-start.1
  5.8 0.0 copy-start.4
  5.8 7.3 %all-to-all-start = ((bf16[8,32,128]{2,1,0:T(8,128)(2,1)}), bf16[8,32,128]{2,1,0:T(8,128)(2,1)S(1)}, u32[]{:S(2)}, u32[]{:S(2)}) async-start(bf16[8,32,128]{2,1,0:T(8,128)(2,1)} %get-tuple-element.21), calls=%async_computation | async-start | bytes 131072 | tf_op jit(solution)/shard_map/all_to_all | solution.py:364
  13.1 0.0 copy-start.5
  13.1 0.0 copy-done
  13.1 0.0 copy-done.1
  13.1 0.0 copy-done.4
  13.1 0.6 %copy-done.5 = s32[1,128]{1,0:T(1,128)S(1)} copy-done((s32[1,128]{1,0:T(1,128)S(1)}, s32[1,128]{1,0:T(1,128)}, u32[]{:S(2)}) %copy-start.5) | copy-done | bytes 536
  13.7 0.0 copy-start.2
  13.7 0.8 %slopes.1 = (bf16[256,1024]{1,0:T(8,128)(2,1)S(1)}, bf16[128,1024]{1,0:T(8,128)(2,1)S(1)}, f32[1024,256]{1,0:T(8,128)S(1)}, f32[1024,256]{1,0:T(8,128)S(1)}, f32[1,128]{1,0:T(1,128)S(1)}) custom-call(bf16[32,128]{1,0:T(8,128)(2,1)S(1)} %get-tuple-element.22.after_ref.pooled_ref, bf16[32,4096]{1,0:T(8,128)(2,1)S(1)} %bitcast.6, ...), custom_call_target="tpu_custom_call" | custom-call | tf_op jit(solution)/shard_map/slopes/pallas_call | solution.py:366
  14.5 0.0 copy-start.3
  14.5 5.4 %all-to-all-done = bf16[8,32,128]{2,1,0:T(8,128)(2,1)S(1)} async-done(((bf16[8,32,128]{2,1,0:T(8,128)(2,1)}), bf16[8,32,128]{2,1,0:T(8,128)(2,1)S(1)}, u32[]{:S(2)}, u32[]{:S(2)}) %all-to-all-start) | async-done | bytes 65568 | tf_op jit(solution)/shard_map/all_to_all | solution.py:364
  20.0 0.0 copy-done.2
  20.0 0.0 copy-done.3
  20.0 2.0 %backward.1 = (bf16[96,4,128]{2,1,0:T(4,128)(2,1)S(1)}, f32[1,16]{1,0:T(1,128)}) custom-call(bf16[256,128]{1,0:T(8,128)(2,1)S(1)} %bitcast.7, f32[1,128]{1,0:T(1,128)S(1)} %get-tuple-element.23.mate_ref, bf16[32,128]{1,0:T(8,128)(2,1)S(1)} %get-tuple-element.22.after_ref.pooled_ref, f32[32,128]{1,0:T(8,128)S(1)} %get-tuple-element.24.mixed_ref, ...), custom_call_target="tpu_custom_call" | custom-call | tf_op jit(solution)/shard_map/backward/pallas_call | solution.py:385
  22.0 9.7 %all_to_all.15.refs_0_ = bf16[96,4,128]{2,1,0:T(4,128)(2,1)S(1)} all-to-all(bf16[96,4,128]{2,1,0:T(4,128)(2,1)S(1)} %get-tuple-element.31), channel_id=1, replica_groups=mesh['vol'=8,'rep'=4] {'vol','rep'}, dimensions={0} | all-to-all | bytes 196608 | tf_op jit(solution)/shard_map/all_to_all | solution.py:401
  31.7 0.1 share.1
  31.7 9.5 %all_to_all.16.grad_ref = bf16[96,4,128]{2,1,0:T(4,128)(2,1)S(1)} all-to-all(bf16[96,4,128]{2,1,0:T(4,128)(2,1)S(1)} %share.1), channel_id=1, replica_groups=mesh['vol'=8,'rep'=4] {'vol','rep'}, dimensions={0} | all-to-all | bytes 196608 | tf_op jit(solution)/shard_map/all_to_all | solution.py:410
  41.2 0.8 %updates.1 = (f32[64,128]{1,0:T(8,128)}, f32[128,128]{1,0:T(8,128)}, f32[128,128]{1,0:T(8,128)}, f32[64,128]{1,0:T(8,128)}) custom-call(bf16[96,4,128]{2,1,0:T(4,128)(2,1)S(1)} %all_to_all.16.grad_ref), custom_call_target="tpu_custom_call" | custom-call | tf_op jit(solution)/shard_map/updates/pallas_call | solution.py:414
Async XLA Ops:
  0.6 12.4 %copy-start = (bf16[1,32,4096]{2,1,0:T(8,128)(2,1)S(1)}, bf16[1,32,4096]{2,1,0:T(8,128)(2,1)}, u32[]{:S(2)}) copy-start(bf16[1,32,4096]{2,1,0:T(8,128)(2,1)} %param.7) | copy-start | bytes 786436
  5.7 7.3 %copy-start.1 = (bf16[128,128]{1,0:T(8,128)(2,1)S(1)}, bf16[128,128]{1,0:T(8,128)(2,1)}, u32[]{:S(2)}) copy-start(bf16[128,128]{1,0:T(8,128)(2,1)} %mix_ref.3) | copy-start | bytes 98308
  5.8 7.3 %copy-start.4 = (bf16[64,128]{1,0:T(8,128)(2,1)S(1)}, bf16[64,128]{1,0:T(8,128)(2,1)}, u32[]{:S(2)}) copy-start(bf16[64,128]{1,0:T(8,128)(2,1)} %stem_ref.1) | copy-start | bytes 49156
  5.8 14.2 %all-to-all-start = ((bf16[8,32,128]{2,1,0:T(8,128)(2,1)}), bf16[8,32,128]{2,1,0:T(8,128)(2,1)S(1)}, u32[]{:S(2)}, u32[]{:S(2)}) async-start(bf16[8,32,128]{2,1,0:T(8,128)(2,1)} %get-tuple-element.21), calls=%async_computation | async-start | bytes 131072 | tf_op jit(solution)/shard_map/all_to_all | solution.py:364
  13.1 0.7 %copy-start.5 = (s32[1,128]{1,0:T(1,128)S(1)}, s32[1,128]{1,0:T(1,128)}, u32[]{:S(2)}) copy-start(s32[1,128]{1,0:T(1,128)} %partner_ref.1) | copy-start | bytes 1540
  13.7 6.3 %copy-start.2 = (bf16[128,128]{1,0:T(8,128)(2,1)S(1)}, bf16[128,128]{1,0:T(8,128)(2,1)}, u32[]{:S(2)}) copy-start(bf16[128,128]{1,0:T(8,128)(2,1)} %out_ref.1) | copy-start | bytes 98308
  14.5 5.5 %copy-start.3 = (bf16[128,64]{0,1:T(8,128)(2,1)S(1)}, bf16[128,64]{0,1:T(8,128)(2,1)}, u32[]{:S(2)}) copy-start(bf16[128,64]{0,1:T(8,128)(2,1)} %param.13) | copy-start | bytes 49156

commit v4 on v3

--- a/solution.py
+++ b/solution.py
@@ -10,7 +10,7 @@
 RMS_EPS = 1e-06
 BF16 = jnp.bfloat16
 F32 = jnp.float32
-GROUP = 4
+GROUP = 16
 
 
 def nn(left, right):
@@ -23,10 +23,6 @@
 
 def tn(left, right):
     return lax.dot_general(left, right, (((0,), (0,)), ((), ())), preferred_element_type=F32)
-
-
-def sigmoid(value):
-    return 0.5 + 0.5 * jnp.tanh(0.5 * value)
 
 
 def split(value):
@@ -53,58 +49,55 @@
 
 
 def forward_kernel(
-    count_ref, cut_hbm, stem_hbm, mix_hbm, out_hbm, proj_hbm,
-    send_ref, pooled_ref, mixed_ref, unit_ref, inv_ref,
-    cut_ref, stem_ref, mix_ref, out_ref, proj_ref, sems, cut_sems,
+    count_ref, cut_hbm, stem_hbm, mix_hbm, out_hbm, proj_hbm, partner_hbm,
+    send_ref, pooled_ref, mixed_ref, unit_ref, inv_ref, hidden_t_ref, patch_t_ref,
+    stem_slope_ref, mix_slope_ref, mate_ref, half_mix_ref, out_ref, proj_ref,
+    cut_ref, stem_ref, mix_ref, partner_ref, sems,
 ):
     nodes = cut_ref.shape[0]
     voxels, channels = stem_ref.shape
     width = 2 * voxels
     blocks = cut_ref.shape[1] // width
-
-    def cut_copy(first):
-        lanes = pl.ds(first * width, min(GROUP, blocks - first) * width)
-        return pltpu.make_async_copy(
-            cut_hbm.at[:, lanes], cut_ref.at[:, lanes], cut_sems.at[first // GROUP]
-        )
-
-    def copy(index, source, target):
-        return pltpu.make_async_copy(source, target, sems.at[index])
-
-    stem_copy = copy(0, stem_hbm, stem_ref)
-    mix_copy = copy(1, mix_hbm, mix_ref)
-    late = (copy(2, out_hbm, out_ref), copy(3, proj_hbm, proj_ref))
-    stem_copy.start()
-    cut_copy(0).start()
-    mix_copy.start()
-    for first in range(GROUP, blocks, GROUP):
-        cut_copy(first).start()
-    for each in late:
+    pairs = (
+        (cut_hbm, cut_ref), (stem_hbm, stem_ref), (mix_hbm, mix_ref),
+        (out_hbm, out_ref), (proj_hbm, proj_ref), (partner_hbm, partner_ref),
+    )
+    copies = [
+        pltpu.make_async_copy(source, target, sems.at[i])
+        for i, (source, target) in enumerate(pairs)
+    ]
+    for each in copies:
         each.start()
-    stem_copy.wait()
-    stem2 = paired(stem_ref[...])
-    mix2 = None
+    for each in copies:
+        each.wait()
+    mate_ref[...] = partner_ref[...].astype(F32)
+    stem2 = paired((stem_ref[...].astype(F32) * 0.5).astype(BF16))
+    mix2 = paired((mix_ref[...].astype(F32) * 0.5).astype(BF16))
+    half_mix_ref[...] = mix2
     hidden_sum = jnp.zeros((nodes, 2 * channels), F32)
     mixed_sum = jnp.zeros((nodes, 2 * channels), F32)
     for first in range(0, blocks, GROUP):
         number = min(GROUP, blocks - first)
-        cut_copy(first).wait()
-        pre_stem = nn(pair_rows(cut_ref, width, first, number), stem2)
-        hidden = (pre_stem * sigmoid(pre_stem)).astype(BF16)
-        if first == 0:
-            mix_copy.wait()
-            mix2 = paired(mix_ref[...])
-        pre_mix = nn(hidden, mix2)
-        mixed = (pre_mix * sigmoid(pre_mix)).astype(BF16)
+        rows = slice(first * nodes, (first + number) * nodes)
+        patches = pair_rows(cut_ref, width, first, number)
+        half = nn(patches, stem2)
+        t = jnp.tanh(half)
+        hidden = half + half * t
+        stem_slope_ref[rows, :] = (1.0 + t) + (hidden - hidden * t)
+        narrow = hidden.astype(BF16)
+        half = nn(narrow, mix2)
+        t = jnp.tanh(half)
+        mixed = half + half * t
+        mix_slope_ref[rows, :] = (1.0 + t) + (mixed - mixed * t)
         for i in range(number):
-            rows = slice(i * nodes, (i + 1) * nodes)
-            hidden_sum = hidden_sum + hidden[rows].astype(F32)
-            mixed_sum = mixed_sum + mixed[rows].astype(F32)
+            part = slice(i * nodes, (i + 1) * nodes)
+            hidden_sum = hidden_sum + hidden[part]
+            mixed_sum = mixed_sum + mixed[part]
+        hidden_t_ref[:, rows] = narrow.T
+        patch_t_ref[:, rows] = patches.T
     hidden_sum = hidden_sum[:, :channels] + hidden_sum[:, channels:]
     mixed_sum = mixed_sum[:, :channels] + mixed_sum[:, channels:]
     high, low = split(mixed_sum)
-    for each in late:
-        each.wait()
     weight = out_ref[...]
     summed = hidden_sum + (nn(high, weight) + nn(low, weight))
     pooled = (summed / (2 * blocks)).astype(BF16)
@@ -121,34 +114,6 @@
     mixed_ref[...] = mixed_sum
     unit_ref[...] = unit
     inv_ref[...] = inv
-
-
-def slope_kernel(
-    after_ref, cut_ref, stem_ref, mix_ref, partner_ref,
-    hidden_t_ref, patch_t_ref, stem_slope_ref, mix_slope_ref, mate_ref,
-):
-    del after_ref
-    mate_ref[...] = partner_ref[...].astype(F32)
-    nodes = cut_ref.shape[0]
-    voxels = stem_ref.shape[0]
-    width = 2 * voxels
-    blocks = cut_ref.shape[1] // width
-    stem2 = paired(stem_ref[...])
-    mix2 = paired(mix_ref[...])
-    for first in range(0, blocks, GROUP):
-        number = min(GROUP, blocks - first)
-        rows = slice(first * nodes, (first + number) * nodes)
-        patches = pair_rows(cut_ref, width, first, number)
-        pre_stem = nn(patches, stem2)
-        sigma = sigmoid(pre_stem)
-        scaled = pre_stem * sigma
-        hidden = scaled.astype(BF16)
-        stem_slope_ref[rows, :] = sigma + scaled * (1.0 - sigma)
-        pre_mix = nn(hidden, mix2)
-        sigma = sigmoid(pre_mix)
-        mix_slope_ref[rows, :] = sigma + pre_mix * sigma * (1.0 - sigma)
-        hidden_t_ref[:, rows] = hidden.T
-        patch_t_ref[:, rows] = patches.T
 
 
 def slot_tables(gathered_ref, embed_dim, max_nodes):
@@ -203,12 +168,13 @@
 
 def backward_kernel(
     gathered_ref, mate_ref, pooled_ref, mixed_ref, unit_ref, inv_ref,
-    hidden_t_ref, patch_t_ref, stem_slope_ref, mix_slope_ref, mix_ref, out_ref, proj_ref, grad_ref, loss_ref,
+    hidden_t_ref, patch_t_ref, stem_slope_ref, mix_slope_ref, half_mix_ref, out_ref, proj_ref,
+    grad_ref, loss_ref,
 ):
     nodes, embed_dim = unit_ref.shape
     slots = gathered_ref.shape[0]
     place = lax.axis_index("vol")
-    channels = mix_ref.shape[0]
+    channels = out_ref.shape[0]
     voxels = patch_t_ref.shape[0] // 2
     blocks = stem_slope_ref.shape[0] // nodes
 
@@ -261,11 +227,11 @@
     d_sum = (nn(d_raw, proj_ref[...]) / (2 * blocks)).astype(BF16)
     high, low = split(mixed_ref[...])
     g_out = tn(high, d_sum) + tn(low, d_sum)
-    d_mixed = nt(d_sum, out_ref[...])
+    d_mixed = 0.5 * nt(d_sum, out_ref[...])
     d_mixed = jnp.concatenate([d_mixed, d_mixed], axis=1)
-    d_pool = d_sum.astype(F32)
+    d_pool = 0.5 * d_sum.astype(F32)
     d_pool = jnp.concatenate([d_pool, d_pool], axis=1)
-    mix2 = paired(mix_ref[...])
+    half_mix = half_mix_ref[...]
 
     g_mix = jnp.zeros((2 * channels, 2 * channels), F32)
     g_stem = jnp.zeros((2 * voxels, 2 * channels), F32)
@@ -281,7 +247,7 @@
             axis=0,
         )
         g_mix = g_mix + nn(hidden_t_ref[:, rows], d_pre_mix)
-        back = nt(d_pre_mix, mix2)
+        back = nt(d_pre_mix, half_mix)
         d_pre_stem = jnp.concatenate(
             [
                 (
@@ -306,7 +272,9 @@
     send_ref[...] = total.reshape(send_ref.shape)
 
 
-def update_kernel(grad_ref, *refs):
+def update_kernel(grad_ref, own_loss_ref, *refs):
+    *refs, loss_ref = refs
+    loss_ref[...] = own_loss_ref[...]
     value = grad_ref[...].astype(F32).reshape(-1, grad_ref.shape[-1])
     start = 0
     for ref in refs:
@@ -319,10 +287,6 @@
 
 def vmem(number):
     return [pl.BlockSpec(memory_space=pltpu.VMEM)] * number
-
-
-def anywhere(number):
-    return [pl.BlockSpec(memory_space=pl.ANY)] * number
 
 
 def hbm(number):
@@ -338,13 +302,13 @@
     voxels, channels = w_stem.shape
     embed_dim = w_proj.shape[1]
     rows = cut.shape[1] // (2 * voxels) * nodes
-    groups = (cut.shape[1] // (2 * voxels) + GROUP - 1) // GROUP
     w_proj = w_proj.T
     weights = (w_stem, w_mix, w_out, w_proj)
     shape = jax.ShapeDtypeStruct
     params = pltpu.CompilerParams(vmem_limit_bytes=(16 << 20) + owners * nodes * 8192)
 
-    send, pooled, mixed_sum, unit, inv = pl.pallas_call(
+    pin = pltpu.with_memory_space_constraint
+    send, *saved = pl.pallas_call(
         forward_kernel,
         out_shape=(
             shape((owners, nodes, 2 * embed_dim), BF16),
@@ -352,31 +316,30 @@
             shape((nodes, channels), F32),
             shape((nodes, embed_dim), F32),
             shape((nodes, 1), F32),
-        ),
-        in_specs=[pl.BlockSpec(memory_space=pltpu.SMEM)] + hbm(5),
-        out_specs=tuple(vmem(5)),
-        scratch_shapes=[pltpu.VMEM(a.shape, BF16) for a in (cut,) + weights]
-        + [pltpu.SemaphoreType.DMA((4,)), pltpu.SemaphoreType.DMA((groups,))],
-        compiler_params=params,
-        name="forward",
-    )(counts, *(pltpu.with_memory_space_constraint(a, pltpu.HBM) for a in (cut, *weights)))
-
-    gathered = lax.all_to_all(send, "vol", 0, 0).reshape(owners * nodes, 2 * embed_dim)
-
-    hidden_t, patch_t, stem_slope, mix_slope, mates = pl.pallas_call(
-        slope_kernel,
-        out_shape=(
             shape((2 * channels, rows), BF16),
             shape((2 * voxels, rows), BF16),
             shape((rows, 2 * channels), F32),
             shape((rows, 2 * channels), F32),
             shape(partner.shape, F32),
+            shape((2 * channels, 2 * channels), BF16),
+            shape(w_out.shape, BF16),
+            shape(w_proj.shape, BF16),
         ),
-        in_specs=anywhere(1) + vmem(4),
-        out_specs=tuple(vmem(5)),
+        in_specs=[pl.BlockSpec(memory_space=pltpu.SMEM)] + hbm(6),
+        out_specs=tuple(vmem(13)),
+        scratch_shapes=[
+            pltpu.VMEM(cut.shape, BF16),
+            pltpu.VMEM(w_stem.shape, BF16),
+            pltpu.VMEM(w_mix.shape, BF16),
+            pltpu.VMEM(partner.shape, jnp.int32),
+            pltpu.SemaphoreType.DMA((6,)),
+        ],
         compiler_params=params,
-        name="slopes",
-    )(pooled, cut, w_stem, w_mix, partner)
+        name="forward",
+    )(counts, *(pin(a, pltpu.HBM) for a in (cut, *weights, partner)))
+    pooled, mixed_sum, unit, inv, hidden_t, patch_t, stem_slope, mix_slope, mates, *rest = saved
+
+    gathered = lax.all_to_all(send, "vol", 0, 0).reshape(owners * nodes, 2 * embed_dim)
 
     total_rows = sum(w.shape[0] for w in weights)
     share = (total_rows + devices - 1) // devices
@@ -394,7 +357,7 @@
         name="backward",
     )(
         gathered, mates, pooled, mixed_sum, unit, inv,
-        hidden_t, patch_t, stem_slope, mix_slope, w_mix, w_out, w_proj,
+        hidden_t, patch_t, stem_slope, mix_slope, *rest,
     )
     if padded:
         parts = jnp.pad(parts, ((0, padded), (0, 0))).reshape(-1, tile, channels)
@@ -413,13 +376,13 @@
 
     updates = pl.pallas_call(
         update_kernel,
-        out_shape=tuple(shape(w.shape, F32) for w in weights),
-        in_specs=vmem(1),
-        out_specs=tuple(vmem(4)),
+        out_shape=tuple(shape(w.shape, F32) for w in weights) + (shape(loss.shape, F32),),
+        in_specs=vmem(2),
+        out_specs=tuple(vmem(5)),
         compiler_params=params,
         name="updates",
-    )(whole)
-    return (*updates[:3], updates[3].T, loss[None])
+    )(whole, loss)
+    return (*updates[:3], updates[3].T, updates[4][None])
 
 
 def solution(mesh):

time: 42.4 us -> 39.3 us (0.927)
  blocking collectives: 19.2 us -> 33.2 us
  starting transfers between devices: 7.29 us -> 0 us
  waiting for transfers between devices: 5.44 us -> 0 us
  Pallas kernels: 8.06 us -> 4.6 us
  local copies, waits for them, and re-layouts: 0.65 us -> 0 us
    all_to_all x0 -> x1, blocking collectives: none -> 14 us  [on_device(): lax.all_to_all(send, 'vol', 0, 0).reshape(owners * nodes, 2 * embed_dim)]
    all_to_all x1 -> x0, starting transfers between devices: 7.29 us -> none  [on_device(): lax.all_to_all(send, 'vol', 0, 0).reshape(owners * nodes, 2 * embed_dim)]
    all_to_all x1 -> x0, waiting for transfers between devices: 5.44 us -> none  [on_device(): lax.all_to_all(send, 'vol', 0, 0).reshape(owners * nodes, 2 * embed_dim)]
    pallas_call x1, Pallas kernels: 4.41 us -> 2.17 us  [on_device(): pl.pallas_call(forward_kernel, out_shape=(shape((owners, nodes, 2 * embed...]
    pallas_call x1 -> x0, Pallas kernels: 0.79 us -> none  [on_device(): pl.pallas_call(slope_kernel, out_shape=(shape((2 * channels, rows), BF16)...]
    unnamed x12 -> x0, local copies, waits for them, and re-layouts: 0.65 us -> none
  transfers between devices with their start and end apart: 1 -> 0, of which waited for: 1 -> 0; matrix products, arithmetic and copies ran while one was open for 0% -> 0% of each run, Pallas kernels for 2% -> 0%
where the time goes in v4:
time: 39.3 us; the launch traced here: 39.1 us
  blocking collectives  33.2 us (84%)
  Pallas kernels  4.6 us (12%)
  between operations  1.3 us (3%)
    all_to_all x1, blocking collectives, on_device(): lax.all_to_all(send, 'vol', 0, 0).reshape(owners * nodes, 2 * embed_dim)  14 us
    all_to_all x1, blocking collectives, on_device(): parts = lax.all_to_all(parts, axes, 0, 0, tiled=True)  9.74 us
    all_to_all x1, blocking collectives, on_device(): whole = lax.all_to_all(whole, axes, 0, 0, tiled=True)  9.48 us
    pallas_call x1, Pallas kernels, on_device(): pl.pallas_call(forward_kernel, out_shape=(shape((owners, nodes, 2 * embed...  2.17 us
    pallas_call x1, Pallas kernels, on_device(): pl.pallas_call(backward_kernel, out_shape=(shape((total_rows, channels) i...  1.56 us
    pallas_call x1, Pallas kernels, on_device(): pl.pallas_call(update_kernel, out_shape=tuple((shape(w.shape, F32) for w...  0.8 us

profile of v4, /device:TPU:0, one launch (start us, length us, event | category | flops | bytes accessed | tf_op | source)
XLA Modules:
  0.0 39.1 jit_solution(16653502533983209446)
XLA Ops:
  1.3 2.2 %forward.1 = (bf16[8,32,128]{2,1,0:T(8,128)(2,1)S(1)}, bf16[32,128]{1,0:T(8,128)(2,1)S(1)}, f32[32,128]{1,0:T(8,128)S(1)}, f32[32,64]{1,0:T(8,128)S(1)}, f32[32,...) custom-call(s32[1,1]{1,0:T(1,128)S(6)} %copy.12.count_ref, ...), custom_call_target="tpu_custom_call" | custom-call | tf_op jit(solution)/shard_map/forward/pallas_call | solution.py:311
  3.5 14.0 %all_to_all.15 = bf16[8,32,128]{2,1,0:T(8,128)(2,1)S(1)} all-to-all(bf16[8,32,128]{2,1,0:T(8,128)(2,1)S(1)} %get-tuple-element.25), channel_id=1, replica_groups=mesh['vol'=8,'rep'=4] {'vol'}, dimensions={0} | all-to-all | bytes 131072 | tf_op jit(solution)/shard_map/all_to_all | solution.py:342
  17.4 1.6 %backward.1 = (bf16[96,4,128]{2,1,0:T(4,128)(2,1)S(1)}, f32[1,16]{1,0:T(1,128)S(1)}) custom-call(bf16[256,128]{1,0:T(8,128)(2,1)S(1)} %bitcast.5, f32[1,128]{1,0:T(1,128)S(1)} %get-tuple-element.26.mate_ref, bf16[32,128]{1,0:T(8,128)(2,1)S(1)} %get-tuple-element.27.pooled_ref, f32[32,128]{1,0:T(8,128)S(1)} %get-tuple-element.28.mixed_ref, ...), custom_call_target="tpu_custom_call" | custom-call | tf_op jit(solution)/shard_map/backward/pallas_call | solution.py:348
  19.0 9.7 %all_to_all.16.refs_0_ = bf16[96,4,128]{2,1,0:T(4,128)(2,1)S(1)} all-to-all(bf16[96,4,128]{2,1,0:T(4,128)(2,1)S(1)} %get-tuple-element.38), channel_id=1, replica_groups=mesh['vol'=8,'rep'=4] {'vol','rep'}, dimensions={0} | all-to-all | bytes 196608 | tf_op jit(solution)/shard_map/all_to_all | solution.py:364
  28.7 0.1 share.1
  28.8 9.5 %all_to_all.17.grad_ref = bf16[96,4,128]{2,1,0:T(4,128)(2,1)S(1)} all-to-all(bf16[96,4,128]{2,1,0:T(4,128)(2,1)S(1)} %share.1), channel_id=1, replica_groups=mesh['vol'=8,'rep'=4] {'vol','rep'}, dimensions={0} | all-to-all | bytes 196608 | tf_op jit(solution)/shard_map/all_to_all | solution.py:373
  38.3 0.8 %updates.1 = (f32[64,128]{1,0:T(8,128)}, f32[128,128]{1,0:T(8,128)}, f32[128,128]{1,0:T(8,128)}, f32[64,128]{1,0:T(8,128)}, f32[1,16]{1,0:T(1,128)}) custom-call(bf16[96,4,128]{2,1,0:T(4,128)(2,1)S(1)} %all_to_all.17.grad_ref, f32[1,16]{1,0:T(1,128)S(1)} %get-tuple-element.39.own_loss_ref), custom_call_target="tpu_custom_call" | custom-call | tf_op jit(solution)/shard_map/updates/pallas_call | solution.py:377

commit v5 on v4

--- a/solution.py
+++ b/solution.py
@@ -48,29 +48,25 @@
     )
 
 
+def first_kernel(first_ref):
+    first_ref[...] = jnp.zeros(first_ref.shape, first_ref.dtype)
+
+
 def forward_kernel(
-    count_ref, cut_hbm, stem_hbm, mix_hbm, out_hbm, proj_hbm, partner_hbm,
+    first_ref, count_ref, cut_ref, stem_ref, mix_ref, out_in, proj_in, partner_hbm,
     send_ref, pooled_ref, mixed_ref, unit_ref, inv_ref, hidden_t_ref, patch_t_ref,
     stem_slope_ref, mix_slope_ref, mate_ref, half_mix_ref, out_ref, proj_ref,
-    cut_ref, stem_ref, mix_ref, partner_ref, sems,
+    partner_ref, sem,
 ):
     nodes = cut_ref.shape[0]
     voxels, channels = stem_ref.shape
     width = 2 * voxels
     blocks = cut_ref.shape[1] // width
-    pairs = (
-        (cut_hbm, cut_ref), (stem_hbm, stem_ref), (mix_hbm, mix_ref),
-        (out_hbm, out_ref), (proj_hbm, proj_ref), (partner_hbm, partner_ref),
-    )
-    copies = [
-        pltpu.make_async_copy(source, target, sems.at[i])
-        for i, (source, target) in enumerate(pairs)
-    ]
-    for each in copies:
-        each.start()
-    for each in copies:
-        each.wait()
-    mate_ref[...] = partner_ref[...].astype(F32)
+    del first_ref
+    out_ref[...] = out_in[...]
+    proj_ref[...] = proj_in[...]
+    partner_copy = pltpu.make_async_copy(partner_hbm, partner_ref, sem)
+    partner_copy.start()
     stem2 = paired((stem_ref[...].astype(F32) * 0.5).astype(BF16))
     mix2 = paired((mix_ref[...].astype(F32) * 0.5).astype(BF16))
     half_mix_ref[...] = mix2
@@ -82,13 +78,15 @@
         patches = pair_rows(cut_ref, width, first, number)
         half = nn(patches, stem2)
         t = jnp.tanh(half)
-        hidden = half + half * t
-        stem_slope_ref[rows, :] = (1.0 + t) + (hidden - hidden * t)
+        u = 1.0 + t
+        hidden = half * u
+        stem_slope_ref[rows, :] = u + hidden * (1.0 - t)
         narrow = hidden.astype(BF16)
         half = nn(narrow, mix2)
         t = jnp.tanh(half)
-        mixed = half + half * t
-        mix_slope_ref[rows, :] = (1.0 + t) + (mixed - mixed * t)
+        u = 1.0 + t
+        mixed = half * u
+        mix_slope_ref[rows, :] = u + mixed * (1.0 - t)
         for i in range(number):
             part = slice(i * nodes, (i + 1) * nodes)
             hidden_sum = hidden_sum + hidden[part]
@@ -110,6 +108,8 @@
     counts = jnp.zeros(unit.shape, F32) + count.astype(F32)
     send = jnp.concatenate([embed, counts], axis=1).astype(BF16)
     send_ref[...] = jnp.broadcast_to(send[None], send_ref.shape)
+    partner_copy.wait()
+    mate_ref[...] = partner_ref[...].astype(F32)
     pooled_ref[...] = pooled
     mixed_ref[...] = mixed_sum
     unit_ref[...] = unit
@@ -307,7 +307,14 @@
     shape = jax.ShapeDtypeStruct
     params = pltpu.CompilerParams(vmem_limit_bytes=(16 << 20) + owners * nodes * 8192)
 
-    pin = pltpu.with_memory_space_constraint
+    first = pl.pallas_call(
+        first_kernel,
+        out_shape=shape((8, 128), F32),
+        out_specs=vmem(1)[0],
+        compiler_params=params,
+        cost_estimate=pl.CostEstimate(flops=10**9, transcendentals=10**6, bytes_accessed=10**8),
+        name="first",
+    )()
     send, *saved = pl.pallas_call(
         forward_kernel,
         out_shape=(
@@ -325,18 +332,12 @@
             shape(w_out.shape, BF16),
             shape(w_proj.shape, BF16),
         ),
-        in_specs=[pl.BlockSpec(memory_space=pltpu.SMEM)] + hbm(6),
+        in_specs=vmem(1) + [pl.BlockSpec(memory_space=pltpu.SMEM)] + vmem(5) + hbm(1),
         out_specs=tuple(vmem(13)),
-        scratch_shapes=[
-            pltpu.VMEM(cut.shape, BF16),
-            pltpu.VMEM(w_stem.shape, BF16),
-            pltpu.VMEM(w_mix.shape, BF16),
-            pltpu.VMEM(partner.shape, jnp.int32),
-            pltpu.SemaphoreType.DMA((6,)),
-        ],
+        scratch_shapes=[pltpu.VMEM(partner.shape, jnp.int32), pltpu.SemaphoreType.DMA(())],
         compiler_params=params,
         name="forward",
-    )(counts, *(pin(a, pltpu.HBM) for a in (cut, *weights, partner)))
+    )(first, counts, cut, *weights, pltpu.with_memory_space_constraint(partner, pltpu.HBM))
     pooled, mixed_sum, unit, inv, hidden_t, patch_t, stem_slope, mix_slope, mates, *rest = saved
 
     gathered = lax.all_to_all(send, "vol", 0, 0).reshape(owners * nodes, 2 * embed_dim)

time: 39.3 us -> 39.1 us (level)
  Pallas kernels: 4.6 us -> 4.03 us
    pallas_call x1, Pallas kernels: 2.17 us -> 1.6 us  [on_device(): pl.pallas_call(forward_kernel, out_shape=(shape((owners, nodes, 2 * embed...]
where the time goes in v5:
time: 39.1 us; the launch traced here: 38.9 us
  blocking collectives  33.2 us (85%)
  Pallas kernels  4.03 us (10%)
  between operations  1.39 us (4%)
    all_to_all x1, blocking collectives, on_device(): lax.all_to_all(send, 'vol', 0, 0).reshape(owners * nodes, 2 * embed_dim)  14 us
    all_to_all x1, blocking collectives, on_device(): parts = lax.all_to_all(parts, axes, 0, 0, tiled=True)  9.74 us
    all_to_all x1, blocking collectives, on_device(): whole = lax.all_to_all(whole, axes, 0, 0, tiled=True)  9.48 us
    pallas_call x1, Pallas kernels, on_device(): pl.pallas_call(forward_kernel, out_shape=(shape((owners, nodes, 2 * embed...  1.6 us
    pallas_call x1, Pallas kernels, on_device(): pl.pallas_call(backward_kernel, out_shape=(shape((total_rows, channels) i...  1.56 us
    pallas_call x1, Pallas kernels, on_device(): pl.pallas_call(update_kernel, out_shape=tuple((shape(w.shape, F32) for w...  0.8 us

profile of v5, /device:TPU:0, one launch (start us, length us, event | category | flops | bytes accessed | tf_op | source)
XLA Modules:
  0.0 38.9 jit_solution(1898207330496606623)
XLA Ops:
  0.6 0.0 copy-start.2
  0.6 0.0 copy-start.1
  0.7 0.0 copy-start
  0.7 0.0 copy-start.3
  0.7 0.0 copy-start.4
  1.4 0.0 copy-done.2
  1.4 0.0 copy-done.1
  1.4 0.2 copy-done
  1.6 0.0 copy-done.3
  1.6 0.0 copy-done.4
  1.6 1.6 %forward.1 = (bf16[8,32,128]{2,1,0:T(8,128)(2,1)S(1)}, bf16[32,128]{1,0:T(8,128)(2,1)S(1)}, f32[32,128]{1,0:T(8,128)S(1)}, f32[32,64]{1,0:T(8,128)S(1)}, f32[32,...) custom-call(f32[8,128]{1,0:T(8,128)S(1)} %first.1.first_ref, ...), custom_call_target="tpu_custom_call" | custom-call | tf_op jit(solution)/shard_map/forward/pallas_call | solution.py:318
  3.2 14.0 %all_to_all.15 = bf16[8,32,128]{2,1,0:T(8,128)(2,1)S(1)} all-to-all(bf16[8,32,128]{2,1,0:T(8,128)(2,1)S(1)} %get-tuple-element.25), channel_id=1, replica_groups=mesh['vol'=8,'rep'=4] {'vol'}, dimensions={0} | all-to-all | bytes 131072 | tf_op jit(solution)/shard_map/all_to_all | solution.py:343
  17.2 1.6 %backward.1 = (bf16[96,4,128]{2,1,0:T(4,128)(2,1)S(1)}, f32[1,16]{1,0:T(1,128)S(1)}) custom-call(bf16[256,128]{1,0:T(8,128)(2,1)S(1)} %bitcast.5, f32[1,128]{1,0:T(1,128)S(1)} %get-tuple-element.26.mate_ref, bf16[32,128]{1,0:T(8,128)(2,1)S(1)} %get-tuple-element.27.pooled_ref, f32[32,128]{1,0:T(8,128)S(1)} %get-tuple-element.28.mixed_ref, ...), custom_call_target="tpu_custom_call" | custom-call | tf_op jit(solution)/shard_map/backward/pallas_call | solution.py:349
  18.8 9.7 %all_to_all.16.refs_0_ = bf16[96,4,128]{2,1,0:T(4,128)(2,1)S(1)} all-to-all(bf16[96,4,128]{2,1,0:T(4,128)(2,1)S(1)} %get-tuple-element.38), channel_id=1, replica_groups=mesh['vol'=8,'rep'=4] {'vol','rep'}, dimensions={0} | all-to-all | bytes 196608 | tf_op jit(solution)/shard_map/all_to_all | solution.py:365
  28.5 0.1 share.1
  28.6 9.5 %all_to_all.17.grad_ref = bf16[96,4,128]{2,1,0:T(4,128)(2,1)S(1)} all-to-all(bf16[96,4,128]{2,1,0:T(4,128)(2,1)S(1)} %share.1), channel_id=1, replica_groups=mesh['vol'=8,'rep'=4] {'vol','rep'}, dimensions={0} | all-to-all | bytes 196608 | tf_op jit(solution)/shard_map/all_to_all | solution.py:374
  38.1 0.8 %updates.1 = (f32[64,128]{1,0:T(8,128)}, f32[128,128]{1,0:T(8,128)}, f32[128,128]{1,0:T(8,128)}, f32[64,128]{1,0:T(8,128)}, f32[1,16]{1,0:T(1,128)}) custom-call(bf16[96,4,128]{2,1,0:T(4,128)(2,1)S(1)} %all_to_all.17.grad_ref, f32[1,16]{1,0:T(1,128)S(1)} %get-tuple-element.39.own_loss_ref), custom_call_target="tpu_custom_call" | custom-call | tf_op jit(solution)/shard_map/updates/pallas_call | solution.py:378
  (1 shorter events, 0.0 us)
Async XLA Ops:
  0.6 0.8 %copy-start.2 = (bf16[128,128]{1,0:T(8,128)(2,1)S(1)}, bf16[128,128]{1,0:T(8,128)(2,1)}, u32[]{:S(2)}) copy-start(bf16[128,128]{1,0:T(8,128)(2,1)} %out_in.1) | copy-start | bytes 98308
  0.6 0.8 %copy-start.1 = (bf16[128,128]{1,0:T(8,128)(2,1)S(1)}, bf16[128,128]{1,0:T(8,128)(2,1)}, u32[]{:S(2)}) copy-start(bf16[128,128]{1,0:T(8,128)(2,1)} %mix_ref.1) | copy-start | bytes 98308
  0.7 1.0 %copy-start = (bf16[1,32,4096]{2,1,0:T(8,128)(2,1)S(1)}, bf16[1,32,4096]{2,1,0:T(8,128)(2,1)}, u32[]{:S(2)}) copy-start(bf16[1,32,4096]{2,1,0:T(8,128)(2,1)} %param.7) | copy-start | bytes 786436
  0.7 1.0 %copy-start.3 = (bf16[64,128]{1,0:T(8,128)(2,1)S(1)}, bf16[64,128]{1,0:T(8,128)(2,1)}, u32[]{:S(2)}) copy-start(bf16[64,128]{1,0:T(8,128)(2,1)} %stem_ref.1) | copy-start | bytes 49156
  0.7 1.0 %copy-start.4 = (bf16[128,64]{0,1:T(8,128)(2,1)S(1)}, bf16[128,64]{0,1:T(8,128)(2,1)}, u32[]{:S(2)}) copy-start(bf16[128,64]{0,1:T(8,128)(2,1)} %param.13) | copy-start | bytes 49156

commit v6 on v5

--- a/solution.py
+++ b/solution.py
@@ -66,7 +66,15 @@
     out_ref[...] = out_in[...]
     proj_ref[...] = proj_in[...]
     partner_copy = pltpu.make_async_copy(partner_hbm, partner_ref, sem)
-    partner_copy.start()
+
+    def begin(step, carry):
+        @pl.when(step == 0)
+        def _():
+            partner_copy.start()
+
+        return carry
+
+    lax.fori_loop(0, 2, begin, 0)
     stem2 = paired((stem_ref[...].astype(F32) * 0.5).astype(BF16))
     mix2 = paired((mix_ref[...].astype(F32) * 0.5).astype(BF16))
     half_mix_ref[...] = mix2
@@ -108,31 +116,30 @@
     counts = jnp.zeros(unit.shape, F32) + count.astype(F32)
     send = jnp.concatenate([embed, counts], axis=1).astype(BF16)
     send_ref[...] = jnp.broadcast_to(send[None], send_ref.shape)
-    partner_copy.wait()
-    mate_ref[...] = partner_ref[...].astype(F32)
     pooled_ref[...] = pooled
     mixed_ref[...] = mixed_sum
     unit_ref[...] = unit
     inv_ref[...] = inv
 
+    partner_copy.wait()
+    mate_ref[...] = partner_ref[...].astype(F32)
+
 
 def slot_tables(gathered_ref, embed_dim, max_nodes):
     slots = gathered_ref.shape[0]
     owners = slots // max_nodes
-    lane = lax.broadcasted_iota(jnp.int32, (8, gathered_ref.shape[1]), 1)
-    pick = jnp.where(lane == embed_dim, 1.0, 0.0).astype(BF16)
-    count = nt(pick, gathered_ref[...])
-    slot = lax.broadcasted_iota(jnp.int32, (8, slots), 1)
-    heads = jnp.where(slot % max_nodes == 0, count, 0.0)
-    step = min(slots, 512)
-    row = lax.broadcasted_iota(jnp.int32, (step, slots), 0)
-    column_owner = lax.broadcasted_iota(jnp.int32, (step, slots), 1) // max_nodes
-    offset = jnp.zeros((8, slots), F32)
-    for first in range(0, slots, step):
-        earlier = jnp.where((row + first) // max_nodes < column_owner, 1.0, 0.0).astype(BF16)
-        offset = offset + nn(heads[:, first : first + step].astype(BF16), earlier)
-    del owners
-    return count[0:1], offset[0:1], heads[0:1]
+    counts = jnp.concatenate(
+        [
+            gathered_ref[i * max_nodes : i * max_nodes + 8, embed_dim : embed_dim + 1].astype(F32)[:1]
+            for i in range(owners)
+        ],
+        axis=0,
+    )
+    owner = lax.broadcasted_iota(jnp.int32, (owners, slots), 0)
+    slot_owner = lax.broadcasted_iota(jnp.int32, (owners, slots), 1) // max_nodes
+    count = jnp.sum(jnp.where(owner == slot_owner, counts, 0.0), axis=0, keepdims=True)
+    offset = jnp.sum(jnp.where(owner < slot_owner, counts, 0.0), axis=0, keepdims=True)
+    return count, offset, counts
 
 
 def score_sums(gathered_ref, embed_dim, max_nodes, live_row):
@@ -178,16 +185,15 @@
     voxels = patch_t_ref.shape[0] // 2
     blocks = stem_slope_ref.shape[0] // nodes
 
-    count_row, offset_row, heads = slot_tables(gathered_ref, embed_dim, nodes)
+    count_row, offset_row, counts = slot_tables(gathered_ref, embed_dim, nodes)
     slot_row = lax.broadcasted_iota(jnp.int32, (1, slots), 1)
     within = (slot_row % nodes).astype(F32)
     live_row = within < count_row
     number_row = jnp.where(live_row, offset_row + within, -1.0)
     totals = score_sums(gathered_ref, embed_dim, nodes, live_row)
 
-    own_offset = jnp.sum(
-        jnp.where(slot_row // nodes < place, heads, 0.0), axis=1, keepdims=True
-    )
+    owner = lax.broadcasted_iota(jnp.int32, counts.shape, 0)
+    own_offset = jnp.sum(jnp.where(owner < place, counts, 0.0), axis=0, keepdims=True)
     rank = lax.broadcasted_iota(jnp.int32, (nodes, 1), 0)
     own_number = own_offset + rank.astype(F32)
     mate = look_up(mate_ref, own_number)

time: 39.1 us -> 38.5 us (0.985)
  Pallas kernels: 4.03 us -> 3.45 us
    pallas_call x1, Pallas kernels: 1.6 us -> 1.12 us  [on_device(): pl.pallas_call(forward_kernel, out_shape=(shape((owners, nodes, 2 * embed...]
where the time goes in v6:
time: 38.5 us; the launch traced here: 38.3 us
  blocking collectives  33.2 us (86%)
  Pallas kernels  3.45 us (9%)
  between operations  1.39 us (4%)
    all_to_all x1, blocking collectives, on_device(): lax.all_to_all(send, 'vol', 0, 0).reshape(owners * nodes, 2 * embed_dim)  14 us
    all_to_all x1, blocking collectives, on_device(): parts = lax.all_to_all(parts, axes, 0, 0, tiled=True)  9.74 us
    all_to_all x1, blocking collectives, on_device(): whole = lax.all_to_all(whole, axes, 0, 0, tiled=True)  9.48 us
    pallas_call x1, Pallas kernels, on_device(): pl.pallas_call(backward_kernel, out_shape=(shape((total_rows, channels) i...  1.45 us
    pallas_call x1, Pallas kernels, on_device(): pl.pallas_call(forward_kernel, out_shape=(shape((owners, nodes, 2 * embed...  1.12 us
    pallas_call x1, Pallas kernels, on_device(): pl.pallas_call(update_kernel, out_shape=tuple((shape(w.shape, F32) for w...  0.8 us

profile of v6, /device:TPU:0, one launch (start us, length us, event | category | flops | bytes accessed | tf_op | source)
XLA Modules:
  0.0 38.3 jit_solution(16527613863857125816)
XLA Ops:
  0.6 0.0 copy-start.2
  0.6 0.0 copy-start.1
  0.7 0.0 copy-start
  0.7 0.0 copy-start.3
  0.7 0.0 copy-start.4
  1.4 0.0 copy-done.2
  1.4 0.0 copy-done.1
  1.4 0.2 copy-done
  1.6 0.0 copy-done.3
  1.6 0.0 copy-done.4
  1.6 1.1 %forward.1 = (bf16[8,32,128]{2,1,0:T(8,128)(2,1)S(1)}, bf16[32,128]{1,0:T(8,128)(2,1)S(1)}, f32[32,128]{1,0:T(8,128)S(1)}, f32[32,64]{1,0:T(8,128)S(1)}, f32[32,...) custom-call(f32[8,128]{1,0:T(8,128)S(1)} %first.1.first_ref, ...), custom_call_target="tpu_custom_call" | custom-call | tf_op jit(solution)/shard_map/forward/pallas_call | solution.py:324
  2.8 14.0 %all_to_all.15 = bf16[8,32,128]{2,1,0:T(8,128)(2,1)S(1)} all-to-all(bf16[8,32,128]{2,1,0:T(8,128)(2,1)S(1)} %get-tuple-element.25), channel_id=1, replica_groups=mesh['vol'=8,'rep'=4] {'vol'}, dimensions={0} | all-to-all | bytes 131072 | tf_op jit(solution)/shard_map/all_to_all | solution.py:349
  16.8 1.5 %backward.1 = (bf16[96,4,128]{2,1,0:T(4,128)(2,1)S(1)}, f32[1,16]{1,0:T(1,128)S(1)}) custom-call(bf16[256,128]{1,0:T(8,128)(2,1)S(1)} %bitcast.5, f32[1,128]{1,0:T(1,128)S(1)} %get-tuple-element.26.mate_ref, bf16[32,128]{1,0:T(8,128)(2,1)S(1)} %get-tuple-element.27.pooled_ref, f32[32,128]{1,0:T(8,128)S(1)} %get-tuple-element.28.mixed_ref, ...), custom_call_target="tpu_custom_call" | custom-call | tf_op jit(solution)/shard_map/backward/pallas_call | solution.py:355
  18.2 9.7 %all_to_all.16.refs_0_ = bf16[96,4,128]{2,1,0:T(4,128)(2,1)S(1)} all-to-all(bf16[96,4,128]{2,1,0:T(4,128)(2,1)S(1)} %get-tuple-element.38), channel_id=1, replica_groups=mesh['vol'=8,'rep'=4] {'vol','rep'}, dimensions={0} | all-to-all | bytes 196608 | tf_op jit(solution)/shard_map/all_to_all | solution.py:371
  28.0 0.1 share.1
  28.0 9.5 %all_to_all.17.grad_ref = bf16[96,4,128]{2,1,0:T(4,128)(2,1)S(1)} all-to-all(bf16[96,4,128]{2,1,0:T(4,128)(2,1)S(1)} %share.1), channel_id=1, replica_groups=mesh['vol'=8,'rep'=4] {'vol','rep'}, dimensions={0} | all-to-all | bytes 196608 | tf_op jit(solution)/shard_map/all_to_all | solution.py:380
  37.5 0.8 %updates.1 = (f32[64,128]{1,0:T(8,128)}, f32[128,128]{1,0:T(8,128)}, f32[128,128]{1,0:T(8,128)}, f32[64,128]{1,0:T(8,128)}, f32[1,16]{1,0:T(1,128)}) custom-call(bf16[96,4,128]{2,1,0:T(4,128)(2,1)S(1)} %all_to_all.17.grad_ref, f32[1,16]{1,0:T(1,128)S(1)} %get-tuple-element.39.own_loss_ref), custom_call_target="tpu_custom_call" | custom-call | tf_op jit(solution)/shard_map/updates/pallas_call | solution.py:384
  (1 shorter events, 0.0 us)
Async XLA Ops:
  0.6 0.8 %copy-start.2 = (bf16[128,128]{1,0:T(8,128)(2,1)S(1)}, bf16[128,128]{1,0:T(8,128)(2,1)}, u32[]{:S(2)}) copy-start(bf16[128,128]{1,0:T(8,128)(2,1)} %out_in.1) | copy-start | bytes 98308
  0.6 0.8 %copy-start.1 = (bf16[128,128]{1,0:T(8,128)(2,1)S(1)}, bf16[128,128]{1,0:T(8,128)(2,1)}, u32[]{:S(2)}) copy-start(bf16[128,128]{1,0:T(8,128)(2,1)} %mix_ref.1) | copy-start | bytes 98308
  0.7 1.0 %copy-start = (bf16[1,32,4096]{2,1,0:T(8,128)(2,1)S(1)}, bf16[1,32,4096]{2,1,0:T(8,128)(2,1)}, u32[]{:S(2)}) copy-start(bf16[1,32,4096]{2,1,0:T(8,128)(2,1)} %param.7) | copy-start | bytes 786436
  0.7 1.0 %copy-start.3 = (bf16[64,128]{1,0:T(8,128)(2,1)S(1)}, bf16[64,128]{1,0:T(8,128)(2,1)}, u32[]{:S(2)}) copy-start(bf16[64,128]{1,0:T(8,128)(2,1)} %stem_ref.1) | copy-start | bytes 49156
  0.7 1.0 %copy-start.4 = (bf16[128,64]{0,1:T(8,128)(2,1)S(1)}, bf16[128,64]{0,1:T(8,128)(2,1)}, u32[]{:S(2)}) copy-start(bf16[128,64]{0,1:T(8,128)(2,1)} %param.13) | copy-start | bytes 49156
